TPU v7x, 32 devices: a whole 2x2x4 slice. The times are simulated.
32 devices in a mesh: clip: 2 (over x), ha: 4 (over z), wa: 4 (over y, core).
Axes of the slice: x: 2, y: 2, z: 4, core: 2. Of those that a mesh axis runs over, the one named last changes fastest.
Arguments:
- latent_cond: bfloat16 [2, 1, 64, 64, 2560], P('clip', None, 'ha', 'wa')
- latent_uncond: bfloat16 [2, 1, 64, 64, 2560], P('clip', None, 'ha', 'wa')
- qkv_weight: bfloat16 [2560, 3840], P(('clip', 'ha', 'wa')), may hold values from -0.125 to 0.125
- cond_pairs: bfloat16 [2, 2, 256, 1280], P('clip', None, ('ha', 'wa')), may hold values from -6 to 6
- guide_mask: int32 [2, 16], P('clip', ('ha', 'wa')), may hold values 0 or 1
- shifts: int32 [2, 2], P('clip'), may hold values from -4 to 4, as said below
- kernel: float32 [3, 3, 1280], replicated, may hold values from -1.2 to 1.2
Outputs:
- refined: bfloat16 [2, 2, 1, 64, 64, 1280], P('clip', None, None, 'ha', 'wa')
Inputs may be any that keep to these rules, and one draw needn't show every extreme that they name: `shifts`: in every draw clip 0 has row shift 4 and column shift -4.
All inputs are finite; a program needn't handle non-finite values. No bound on the sum of `guide_mask` on one device may be relied on, other than what follows from the above.
Results may differ from a plain program's by a relative error of at most 0.011.
Values may be sent and summed in bfloat16 or wider, within the bound.
No kernel may reach another device: no remote copies, remote signals or barrier semaphores. Data moves between devices by JAX's collectives and lax.ppermute only.
A program may use at most 128 MiB of HBM per device.

v0:
```python
import functools
import math

import jax
import jax.numpy as jnp
from jax import lax
from jax.experimental import pallas as pl
from jax.experimental.pallas import tpu as pltpu
from jax.sharding import Mesh
from jax.sharding import PartitionSpec as P


HD = 128
WIN = 8
RIM = WIN // 2
CHUNKS = (3, 2)


def cyc(x, axis, step):
    count = lax.axis_size(axis)
    return lax.ppermute(x, axis, [(i, (i + step) % count) for i in range(count)])


def ordered(flag, mine, other, axis):
    first = jnp.where(flag == 0, mine, other)
    second = jnp.where(flag == 0, other, mine)
    return jnp.concatenate([first, second], axis=axis)


def halves_kernel(core_ref, w_ref, mine_ref, other_ref, *, heads, chunks):
    half = heads // 2
    for ref, core in ((mine_ref, core_ref[0]), (other_ref, 1 - core_ref[0])):
        first, at = 0, 0
        for count in chunks:
            for kind in range(ref.shape[1] // (half * HD)):
                start = pl.multiple_of((kind * heads + core * half + first) * HD, HD)
                ref[:, at : at + count * HD] = w_ref[:, pl.ds(start, count * HD)]
                at += count * HD
            first += count


def core_halves(block, heads, chunks):
    rows, cols = block.shape
    half = jax.ShapeDtypeStruct((rows, cols // 2), block.dtype)
    core = lax.axis_index("core").reshape(1)
    return pl.pallas_call(
        functools.partial(halves_kernel, heads=heads, chunks=chunks),
        in_specs=[
            pl.BlockSpec(memory_space=pltpu.SMEM),
            pl.BlockSpec(memory_space=pltpu.VMEM),
        ],
        out_specs=[pl.BlockSpec(memory_space=pltpu.VMEM)] * 2,
        out_shape=[half, half],
        cost_estimate=pl.CostEstimate(flops=0, transcendentals=0, bytes_accessed=4 * block.size),
    )(core, block)


def along_line(block, axis):
    count = lax.axis_size(axis)
    if count != 4:
        near = [cyc(block, axis, d) for d in range(1, count)]
        return near, near[-1]
    steps = {1: [(0, 1), (1, 2), (2, 3)], 2: [(i, (i + 2) % 4) for i in range(4)]}
    steps[3] = [(b, a) for a, b in steps[1]]
    got = {}
    for d, pairs in steps.items():
        got[d] = lax.ppermute(block, axis, pairs)
    passed = lax.ppermute(got[2], axis, [(1, 0), (2, 3)])
    place = lax.axis_index(axis)
    first = jnp.where(place == 0, passed, got[1])
    third = jnp.where(place == 3, passed, got[3])
    return [first, got[2], third], got[2]


def weight_pieces(block, tag, chips):
    side, has = block.shape[0], lax.axis_size("ha")
    if chips != (2, 2):
        full = lax.all_gather(block, ("clip", "ha", "wy"), axis=0, tiled=True)
        return [full], None, side, full[:1]
    near, early = along_line(block, "ha")
    x_own, y_own = cyc(block, "clip", 1), cyc(block, "wy", 1)
    rest = jnp.concatenate(near, axis=0)
    x_rest, y_rest = cyc(rest, "clip", 1), cyc(rest, "wy", 1)
    total = has * side
    mid = 0 if tag == "a" else rest.shape[0] // 2
    arrays = [block, rest, x_own, x_rest, y_own, y_rest, cyc(x_own, "wy", 1)]
    if mid:
        arrays.append(cyc(x_rest[:mid], "wy", 1))
    arrays.append(cyc(y_rest[mid:], "clip", 1))
    pieces = []

    def add(array, begin, end, other_clip, other_wy):
        row = begin
        while row < end:
            d, skip = divmod(row, side)
            stop = min(end, (d + 1) * side)
            pieces.append((array, row - begin, stop - row, other_clip, d, other_wy, skip))
            row = stop

    for k, (oc, oy) in enumerate(((0, 0), (1, 0), (0, 1))):
        add(2 * k, 0, side, oc, oy)
        add(2 * k + 1, side, total, oc, oy)
    add(6, 0, side, 1, 1)
    if mid:
        add(7, side, side + mid, 1, 1)
    add(len(arrays) - 1, side + mid, total, 1, 1)
    return arrays, pieces, side, early


def project_kernel(place, tok_ref, *refs, pieces, side, has):
    arrays, (out_ref, full, sems) = refs[:-3], refs[-3:]
    copies = []
    for k, (array, begin, count, other_clip, d, other_wy, skip) in enumerate(pieces):
        clip = 1 - place[0] if other_clip else place[0]
        wy = 1 - place[2] if other_wy else place[2]
        ha = lax.rem(place[1] + (has - d), has)
        at = pl.multiple_of(((clip * has + ha) * 2 + wy) * side + skip, 16)
        copies.append(
            pltpu.make_async_copy(
                arrays[array].at[pl.ds(begin, count)], full.at[pl.ds(at, count)], sems.at[k]
            )
        )
    for copy in copies:
        copy.start()
    for copy in copies:
        copy.wait()

    @pl.loop(0, tok_ref.shape[0] // 256)
    def _(step):
        rows = pl.ds(pl.multiple_of(step * 256, 256), 256)
        out_ref[rows, :] = jnp.dot(
            tok_ref[rows, :], full[...], preferred_element_type=jnp.float32
        ).astype(out_ref.dtype)


def project(place, tokens, arrays, pieces, side):
    rows, width = tokens.shape
    cols = arrays[0].shape[1]
    if pieces is None:
        return jnp.dot(tokens, arrays[0], preferred_element_type=jnp.float32).astype(tokens.dtype)
    vmem = pl.BlockSpec(memory_space=pltpu.VMEM)
    return pl.pallas_call(
        functools.partial(
            project_kernel, pieces=tuple(pieces), side=side, has=lax.axis_size("ha")
        ),
        in_specs=[pl.BlockSpec(memory_space=pltpu.SMEM), vmem]
        + [pl.BlockSpec(memory_space=pl.ANY)] * len(arrays),
        out_specs=vmem,
        out_shape=jax.ShapeDtypeStruct((rows, cols), jnp.bfloat16),
        scratch_shapes=[
            pltpu.VMEM((width, cols), jnp.bfloat16),
            pltpu.SemaphoreType.DMA((len(pieces),)),
        ],
        cost_estimate=pl.CostEstimate(
            flops=2 * rows * width * cols, transcendentals=0, bytes_accessed=2 * width * cols
        ),
    )(place, tokens, *arrays)


def gathered_pairs(pairs, heads):
    kinds, _, _ = pairs.shape
    block = jnp.concatenate([pairs[k] for k in range(kinds)], axis=1)
    mine, other = core_halves(block, heads, (heads // 2,))
    both = jnp.concatenate([mine, cyc(other, "core", 1)], axis=0)
    steps = range(1, lax.axis_size("wy"))
    both = jnp.concatenate([both] + [cyc(both, "wy", d) for d in steps], axis=0)
    return [both] + [cyc(both, "ha", d) for d in range(1, lax.axis_size("ha"))]


def attend_kernel(info, q_ref, k_ref, v_ref, *refs, width):
    far_refs, (out_ref, bias_ref) = refs[:-2], refs[-2:]
    count = len(far_refs) // 2
    far_keys = jnp.concatenate([ref[...] for ref in far_refs[:count]], axis=0)
    far_values = jnp.concatenate([ref[...] for ref in far_refs[count:]], axis=0)
    rate = math.log2(math.e) / math.sqrt(HD)
    tokens = bias_ref.shape[0]
    shift = info[0]

    def window(shape, axis):
        slot = lax.broadcasted_iota(jnp.int32, shape, axis) & (width - 1)
        return ((slot - shift) & (width - 1)) >> 3

    @pl.when(pl.program_id(0) == 0)
    def _():
        same = window((tokens, tokens), 0) == window((tokens, tokens), 1)
        bias_ref[...] = jnp.where(same, 0.0, -jnp.inf)

    def product(a, b):
        return lax.dot_general(
            a, b, (((1,), (1,)), ((), ())), preferred_element_type=jnp.float32
        )

    def weighted(exps, values):
        ones = jnp.ones_like(values)
        return jnp.dot(
            exps.astype(jnp.bfloat16),
            jnp.concatenate([values, ones], axis=1),
            preferred_element_type=jnp.float32,
        )

    for part in range(4):
        rows = slice(part * tokens, (part + 1) * tokens)
        q = q_ref[rows, :]
        near = product(q, k_ref[rows, :]) + bias_ref[...]
        top = jnp.max(near, axis=-1, keepdims=True)
        if part < 2:
            far = product(q, far_keys)
            top = jnp.maximum(top, jnp.max(far, axis=-1, keepdims=True))
        mixed = weighted(jnp.exp2((near - top) * rate), v_ref[rows, :])
        if part < 2:
            mixed = mixed + weighted(jnp.exp2((far - top) * rate), far_values)
        result = mixed[:, :HD] / mixed[:, HD:]
        if part >= 2:
            keep = jnp.where(window((tokens, 1), 0) < width // 16, info[1], info[2]) > 0
            result = jnp.where(keep, result, 0.0)
        out_ref[rows, :] = result.astype(out_ref.dtype)


def attend(info, projected, far, first, count, width):
    total = projected.shape[0]
    tokens = total // 4
    all_heads = far[0].shape[1] // (2 * HD)
    far_rows = sum(part.shape[0] for part in far)

    def near_spec(offset):
        return pl.BlockSpec((total, HD), lambda i, s: (0, offset + i))

    def far_specs(offset):
        def at(i, s):
            return 0, offset + first + i

        return [pl.BlockSpec((part.shape[0], HD), at) for part in far]

    keys = 2 * tokens + 2 * far_rows
    return pl.pallas_call(
        functools.partial(attend_kernel, width=width),
        grid_spec=pltpu.PrefetchScalarGridSpec(
            num_scalar_prefetch=1,
            grid=(count,),
            in_specs=[
                near_spec(0),
                near_spec(count),
                near_spec(2 * count),
            ]
            + far_specs(0)
            + far_specs(all_heads),
            out_specs=pl.BlockSpec((total, HD), lambda i, s: (0, i)),
            scratch_shapes=[pltpu.VMEM((tokens, tokens), jnp.float32)],
        ),
        out_shape=jax.ShapeDtypeStruct((total, count * HD), jnp.bfloat16),
        cost_estimate=pl.CostEstimate(
            flops=8 * count * tokens * keys * HD,
            transcendentals=2 * count * tokens * keys,
            bytes_accessed=8 * total * count * HD,
        ),
    )(info, projected, projected, projected, *far, *far)


def rows_kernel(info, mine_ref, other_ref, *refs):
    halves, (out_ref, sems) = (refs[:4], refs[4:8]), refs[8:]
    rows, cols = refs[0].shape[:2]
    rim = refs[2].shape[1]

    def copy(source, branch, row, half, sem):
        core = info[1] if half == 0 else 1 - info[1]
        at = pl.multiple_of(core * cols, cols)
        return pltpu.make_async_copy(source, out_ref.at[branch, row, pl.ds(at, cols)], sem)

    def each(row, act):
        start = info[0] + row
        for half, (cond, uncond, above, below) in enumerate(halves):
            for branch, own in enumerate((cond, uncond)):
                sem = sems.at[row, 2 * half + branch]

                @pl.when(start < 0)
                def _():
                    act(copy(above.at[branch, jnp.clip(start + rim, 0, rim - 1)], branch, row, half, sem))

                @pl.when(start >= rows)
                def _():
                    act(copy(below.at[branch, jnp.clip(start - rows, 0, rim - 1)], branch, row, half, sem))

                @pl.when((start >= 0) & (start < rows))
                def _():
                    act(copy(own.at[jnp.clip(start, 0, rows - 1)], branch, row, half, sem))

    @pl.loop(0, rows)
    def _(row):
        each(row, lambda copy: copy.start())

    shift = info[2]
    first = pl.multiple_of(jnp.where(shift > 0, 0, 2 * cols - WIN), WIN)
    own_edge = (shift > 0) == (info[1] == 0)

    @pl.loop(0, rows)
    def _(row):
        each(row, lambda copy: copy.wait())
        slot = lax.broadcasted_iota(jnp.int32, (WIN, out_ref.shape[3]), 0)
        taken = jnp.where(shift > 0, slot - shift, WIN + shift - 1 - slot) < 0
        for branch in range(2):
            edge = jnp.where(own_edge, mine_ref[branch, row], other_ref[branch, row])
            edge = edge.astype(jnp.float32)
            place = pl.ds(first, WIN)
            held = out_ref[branch, row, place].astype(jnp.float32)
            both = jnp.concatenate([edge, edge], axis=0)
            out_ref[branch, row, place] = jnp.where(taken, both, held).astype(out_ref.dtype)


def shifted_tokens(lat_cond, lat_uncond, shift_rows, shift_cols, after):
    core = lax.axis_index("core")
    rows, cols, width = lat_cond.shape
    pair = [lat_cond, lat_uncond]
    late = list(lax.optimization_barrier((lat_cond, lat_uncond, after))[:2])
    twin = [cyc(lat_cond, "core", 1), cyc(lat_uncond, "core", 1)]
    above = cyc(jnp.stack([x[rows - RIM :] for x in late]), "ha", 1)
    below = cyc(jnp.stack([x[:RIM] for x in late]), "ha", -1)
    halves = pair + [above, below]
    halves += twin + [cyc(above, "core", 1), cyc(below, "core", 1)]
    low = jnp.stack([x[:, :RIM] for x in late]), above[:, :, :RIM], below[:, :, :RIM]
    high = [jnp.stack([x[:, cols - RIM :] for x in late])]
    high += [above[:, :, cols - RIM :], below[:, :, cols - RIM :]]
    own, up, dn = (jnp.where(core == 0, a, b) for a, b in zip(low, high))
    tall = jnp.concatenate([up, own, dn], axis=1)
    edge = lax.dynamic_slice_in_dim(tall, RIM + shift_rows, rows, axis=1)
    mine = cyc(edge, "wy", 1)
    other = cyc(mine, "core", 1)
    return pl.pallas_call(
        rows_kernel,
        in_specs=[pl.BlockSpec(memory_space=pltpu.SMEM)]
        + [pl.BlockSpec(memory_space=pltpu.VMEM)] * 2
        + [pl.BlockSpec(memory_space=pl.ANY)] * len(halves),
        out_specs=pl.BlockSpec(memory_space=pltpu.VMEM),
        out_shape=jax.ShapeDtypeStruct((2, rows, 2 * cols, width), lat_cond.dtype),
        scratch_shapes=[pltpu.SemaphoreType.DMA((rows, 4))],
        cost_estimate=pl.CostEstimate(
            flops=0, transcendentals=0, bytes_accessed=16 * rows * cols * width
        ),
    )(jnp.stack([shift_rows, core, shift_cols]), mine, other, *halves)


def refined_part(attended, taps, shift_rows, shift_cols):
    _, rows, cols, _ = attended.shape
    rim = RIM + 1
    above = cyc(attended[:, rows - rim :], "ha", 1)
    below = cyc(attended[:, :rim], "ha", -1)
    tall = jnp.concatenate([above, attended, below], axis=1)
    tall = lax.dynamic_slice_in_dim(tall, RIM - shift_rows, rows + 2, axis=1)
    ha, wy = lax.axis_index("ha"), lax.axis_index("wy")
    row = lax.broadcasted_iota(jnp.int32, (1, rows + 2, 1, 1), 1)
    inside = ((row > 0) | (ha > 0)) & ((row < rows + 1) | (ha < lax.axis_size("ha") - 1))
    tall = jnp.where(inside, tall, jnp.zeros_like(tall))
    first, last = tall[:, :, :1], tall[:, :, cols - 1 :]
    sent = jnp.where(
        shift_cols >= 0,
        jnp.concatenate([tall[:, :, :RIM], last], axis=2),
        jnp.concatenate([tall[:, :, cols - RIM :], first], axis=2),
    )
    got = cyc(sent, "wy", 1)
    blank = jnp.zeros(tall.shape[:2] + (cols - 2 * RIM,) + tall.shape[3:], tall.dtype)
    spread = jnp.concatenate([got[:, :, :RIM], blank, got[:, :, :RIM]], axis=2)
    slot = lax.broadcasted_iota(jnp.int32, (1, 1, cols, 1), 2)
    centre = jnp.where((slot < shift_cols) | (slot >= cols + shift_cols), spread, tall)
    left = jnp.where(shift_cols < 0, last, got[:, :, RIM:])
    right = jnp.where(
        shift_cols > 0, first, jnp.where(shift_cols < 0, got[:, :, RIM:], got[:, :, :1])
    )
    left = jnp.where(wy > 0, left, jnp.zeros_like(left))
    right = jnp.where(wy < lax.axis_size("wy") - 1, right, jnp.zeros_like(right))
    wide = jnp.concatenate([left, centre, right], axis=2)
    summed = wide[:, 1 : rows + 1, 1 : cols + 1].astype(jnp.float32)
    for i in range(3):
        for j in range(3):
            part = wide[:, i : i + rows, j : j + cols].astype(jnp.float32)
            summed = summed + taps[i, j] * part
    return summed.astype(jnp.bfloat16)


def on_device(latent_cond, latent_uncond, qkv_weight, cond_pairs, guide_mask, shifts, kernel):
    _, frames, rows, cols, width_d = latent_cond.shape
    assert frames == 1 and rows == 2 * WIN
    heads = qkv_weight.shape[1] // (3 * HD)
    core = lax.axis_index("core")
    shift_rows, shift_cols = shifts[0, 0], shifts[0, 1]
    own_flag = guide_mask[0]
    flags = ordered(core, own_flag, cyc(own_flag, "core", 1), 0)
    info = jnp.concatenate([shifts[0, 1:], flags])
    place = jnp.stack([lax.axis_index(a) for a in ("clip", "ha", "wy")])
    mine, other = core_halves(qkv_weight, heads, CHUNKS)
    block = ordered(core, mine, cyc(other, "core", 1), 0)
    chips = (lax.axis_size("clip"), lax.axis_size("wy"))
    firsts = [sum(CHUNKS[:i]) for i in range(len(CHUNKS))]
    tags = "abcde"[: len(CHUNKS)]
    held = (block, latent_cond, latent_uncond, cond_pairs)
    block, latent_cond, latent_uncond, cond_pairs = lax.optimization_barrier(held)
    weights = []
    for tag, first, count in zip(tags, firsts, CHUNKS):
        columns = block[:, 3 * first * HD : 3 * (first + count) * HD]
        weights.append(weight_pieces(columns, tag, chips))
    tokens = shifted_tokens(
        latent_cond[0, 0], latent_uncond[0, 0], shift_rows, shift_cols, weights[0][3]
    )
    tokens = tokens.reshape(-1, width_d)
    far = gathered_pairs(cond_pairs[0], heads)
    parts, others = [], []
    for tag, first, count, weight in zip(tags, firsts, CHUNKS, weights):
        projected = project(place, tokens, *weight[:3])
        attended = attend(info, projected, far, first, count, 2 * cols)
        attended = attended.reshape(2, rows, 2 * cols, count * HD)
        taps = lax.dynamic_slice_in_dim(
            kernel, (core * (heads // 2) + first) * HD, count * HD, axis=2
        )
        part = refined_part(attended, taps, shift_rows, shift_cols)
        low, high = part[:, :, :cols], part[:, :, cols:]
        parts.append(jnp.where(core == 0, low, high))
        others.append(cyc(jnp.where(core == 0, high, low), "core", 1))
    out = ordered(core, jnp.concatenate(parts, -1), jnp.concatenate(others, -1), -1)
    return out[None, :, None]


def solution(mesh):
    clips, has, was = (mesh.shape[a] for a in ("clip", "ha", "wa"))
    split = Mesh(mesh.devices.reshape(clips, has, was // 2, 2), ("clip", "ha", "wy", "core"))
    wa = ("wy", "core")
    placed = (
        P("clip", None, "ha", wa, None),
        P("clip", None, "ha", wa, None),
        P(("clip", "ha") + wa, None),
        P("clip", None, ("ha",) + wa, None),
        P("clip", ("ha",) + wa),
        P("clip", None),
        P(),
    )

    return jax.shard_map(
        on_device,
        mesh=split,
        in_specs=placed,
        out_specs=P("clip", None, None, "ha", wa, None),
        check_vma=False,
    )
```

profile of v0, /device:TPU:1, one launch (start us, length us, event | category | flops | bytes accessed | tf_op | source)
XLA Modules:
  0.0 276.3 jit_solution(1212081998926985351)
XLA Ops:
  5.0 3.5 %collective-permute-start.2 = (bf16[160,1152]{1,0:T(8,128)(2,1)S(1)}, bf16[160,1152]{1,0:T(8,128)(2,1)S(1)}, u32[]{:S(2)}, u32[]{:S(2)}) collective-permute-start(bf16[160,1152]{1,0:T(8,128)(2,1)S(1)} %slice.257.refs_0_), channel_id=1, source_target_pairs={{0,8},{4,12},{8,0},{12,4},{1,9},{5,13},{9,1},{13,5},{2,10},{6,14},... | collective-permute-start | bytes 1105928 | tf_op jit(solution)/shard_map/ppermute | solution.py:67
  13.8 3.3 %collective-permute-start.30 = (bf16[160,768]{1,0:T(8,128)(2,1)}, bf16[160,768]{1,0:T(8,128)(2,1)S(1)}, u32[]{:S(2)}, u32[]{:S(2)}) collective-permute-start(bf16[160,768]{1,0:T(8,128)(2,1)} %slice.301.refs_0_), channel_id=1, source_target_pairs={{0,4},{4,8},{8,12},{1,5},{5,9},{9,13},{2,6},{6,10},{10,14},{3,7},{... | collective-permute-start | bytes 737288 | tf_op jit(solution)/shard_map/ppermute | solution.py:67
  19.1 16.5 %collective-permute-done.28 = bf16[160,768]{1,0:T(8,128)(2,1)} collective-permute-done((bf16[160,768]{1,0:T(8,128)(2,1)}, bf16[160,768]{1,0:T(8,128)(2,1)}, u32[]{:S(2)}, u32[]{:S(2)}) %collective-permute-start.28) | collective-permute-done | bytes 245792 | tf_op jit(solution)/shard_map/ppermute | solution.py:67
  40.9 4.7 %collective-permute-start.12 = (bf16[160,1152]{1,0:T(8,128)(2,1)S(1)}, bf16[160,1152]{1,0:T(8,128)(2,1)S(1)}, u32[]{:S(2)}, u32[]{:S(2)}) collective-permute-start(bf16[160,1152]{1,0:T(8,128)(2,1)S(1)} %copy-done.13), channel_id=1, source_target_pairs={{0,4},{4,8},{8,12},{1,5},{5,9},{9,13},{2,6},{6,10},{10,14},{3,7},{... | collective-permute-start | bytes 1105928 | tf_op jit(solution)/shard_map/ppermute | solution.py:67
  47.0 10.2 %collective-permute-done.29 = bf16[160,768]{1,0:T(8,128)(2,1)S(1)} collective-permute-done((bf16[160,768]{1,0:T(8,128)(2,1)}, bf16[160,768]{1,0:T(8,128)(2,1)S(1)}, u32[]{:S(2)}, u32[]{:S(2)}) %collective-permute-start.29) | collective-permute-done | bytes 245792 | tf_op jit(solution)/shard_map/ppermute | solution.py:68
  59.1 3.4 %collective-permute-start.4 = (bf16[2,4,16,2560]{3,2,1,0:T(8,128)(2,1)S(1)}, bf16[2,4,16,2560]{3,2,1,0:T(8,128)(2,1)S(1)}, u32[]{:S(2)}, u32[]{:S(2)}) collective-permute-start(bf16[2,4,16,2560]{3,2,1,0:T(8,128)(2,1)S(1)} %pad_maximum_fusion.5), channel_id=1, source_target_pairs={{0,12},{4,0},{8,4},{12,8},{1,13},{5,1},{9,5},{13,9},{2,14},{6,2},{... | collective-permute-start | bytes 1966088 | tf_op jit(solution)/shard_map/ppermute | solution.py:21
  62.6 17.1 %collective-permute-done.4.refs_3_ = bf16[2,4,16,2560]{3,2,1,0:T(8,128)(2,1)S(1)} collective-permute-done((bf16[2,4,16,2560]{3,2,1,0:T(8,128)(2,1)S(1)}, bf16[2,4,16,2560]{3,2,1,0:T(8,128)(2,1)S(1)}, u32[]{:S(2)}, u32[]{:S(2)}) %collective-permute-start.4) | collective-permute-done | bytes 655392 | tf_op jit(solution)/shard_map/ppermute | solution.py:21
  87.6 4.3 %collective-permute-start.7 = (bf16[16,16,2560]{2,1,0:T(8,128)(2,1)S(1)}, bf16[16,16,2560]{2,1,0:T(8,128)(2,1)}, u32[]{:S(2)}, u32[]{:S(2)}) collective-permute-start(bf16[16,16,2560]{2,1,0:T(8,128)(2,1)S(1)} %bitcast.62), channel_id=1, source_target_pairs={{0,1},{1,0},{2,3},{3,2},{4,5},{5,4},{6,7},{7,6},{8,9},{9,8},{10,11... | collective-permute-start | bytes 3932168 | tf_op jit(solution)/shard_map/ppermute | solution.py:21
  95.0 5.0 %collective-permute-start.8 = (bf16[16,16,2560]{2,1,0:T(8,128)(2,1)S(1)}, bf16[16,16,2560]{2,1,0:T(8,128)(2,1)}, u32[]{:S(2)}, u32[]{:S(2)}) collective-permute-start(bf16[16,16,2560]{2,1,0:T(8,128)(2,1)S(1)} %bitcast.58), channel_id=1, source_target_pairs={{0,1},{1,0},{2,3},{3,2},{4,5},{5,4},{6,7},{7,6},{8,9},{9,8},{10,11... | collective-permute-start | bytes 3932168 | tf_op jit(solution)/shard_map/ppermute | solution.py:21
  106.4 5.7 %collective-permute-done.5.mine_ref = bf16[2,16,4,2560]{3,2,1,0:T(4,128)(2,1)} collective-permute-done((bf16[2,16,4,2560]{3,2,1,0:T(4,128)(2,1)}, bf16[2,16,4,2560]{3,2,1,0:T(4,128)(2,1)}, u32[]{:S(2)}, u32[]{:S(2)}) %collective-permute-start.5) | collective-permute-done | bytes 655392 | tf_op jit(solution)/shard_map/ppermute | solution.py:21
  112.1 4.4 %collective-permute-start.6 = (bf16[2,16,4,2560]{3,2,1,0:T(4,128)(2,1)}, bf16[2,16,4,2560]{3,2,1,0:T(4,128)(2,1)S(1)}, u32[]{:S(2)}, u32[]{:S(2)}) collective-permute-start(bf16[2,16,4,2560]{3,2,1,0:T(4,128)(2,1)} %collective-permute-done.5.mine_ref), channel_id=1, source_target_pairs={{0,1},{1,0},{2,3},{3,2},{4,5},{5,4},{6,7},{7,6},{8,9},{9,8},{10,11... | collective-permute-start | bytes 1966088 | tf_op jit(solution)/shard_map/ppermute | solution.py:21
  126.1 6.9 %shard_map.74 = bf16[2,16,32,2560]{3,2,1,0:T(8,128)(2,1)} custom-call(s32[3]{0:T(128)} %pad_add_fusion.2.info, bf16[2,16,4,2560]{3,2,1,0:T(4,128)(2,1)} %collective-permute-done.5.mine_ref, bf16[2,16,4,2560]{3,2,1,0:T(4,128)(2,1)} %copy-done.11, bf16[16,16,2560]{2,1,0:T(8,128)(2,1)} %bitcast.59, bf16[16,16,2560]{2,1,0:T(8,128)(2,1)} %bitcast.55, ...), custom_call_target="tpu_custom_call" | custom-call | bytes 10485760 | tf_op jit(solution)/shard_map/pallas_call | solution.py:327
  133.1 17.1 %collective-permute-done.34.refs_4_ = bf16[160,768]{1,0:T(8,128)(2,1)S(1)} collective-permute-done((bf16[160,768]{1,0:T(8,128)(2,1)S(1)}, bf16[160,768]{1,0:T(8,128)(2,1)S(1)}, u32[]{:S(2)}, u32[]{:S(2)}) %collective-permute-start.34) | collective-permute-done | bytes 245792 | tf_op jit(solution)/shard_map/ppermute | solution.py:21
  151.2 4.3 %collective-permute-done.36.refs_6_ = bf16[160,768]{1,0:T(8,128)(2,1)S(1)} collective-permute-done((bf16[160,768]{1,0:T(8,128)(2,1)}, bf16[160,768]{1,0:T(8,128)(2,1)S(1)}, u32[]{:S(2)}, u32[]{:S(2)}) %collective-permute-start.36) | collective-permute-done | bytes 245792 | tf_op jit(solution)/shard_map/ppermute | solution.py:21
  155.5 7.9 %collective-permute-done.37.refs_7_ = bf16[240,768]{1,0:T(8,128)(2,1)S(1)} collective-permute-done((bf16[240,768]{1,0:T(8,128)(2,1)S(1)}, bf16[240,768]{1,0:T(8,128)(2,1)S(1)}, u32[]{:S(2)}, u32[]{:S(2)}) %collective-permute-start.37) | collective-permute-done | bytes 368672 | tf_op jit(solution)/shard_map/ppermute | solution.py:21
  164.9 10.7 %shard_map.78.q_ref.k_ref.v_ref = bf16[1024,768]{1,0:T(8,128)(2,1)} custom-call(s32[3]{0:T(128)} %pad_add_fusion.1.place, bf16[1024,2560]{1,0:T(8,128)(2,1)} %bitcast.53, bf16[160,768]{1,0:T(8,128)(2,1)} %slice.301.refs_0_, bf16[480,768]{1,0:T(8,128)(2,1)} %pad_maximum_fusion.3.refs_1_, bf16[160,768]{1,0:T(8,128)(2,1)} %collective-permute-done.32.refs_2_, ...), custom_call_target="tpu_custom_call" | custom-call | flops 4026531840 | bytes 3932160 | tf_op jit(solution)/shard_map/pallas_call | solution.py:142
  178.5 4.6 %shard_map.79 = bf16[1024,256]{1,0:T(8,128)(2,1)} custom-call(s32[3]{0:T(128)} %pad_add_fusion.info, bf16[1024,768]{1,0:T(8,128)(2,1)} %shard_map.78.q_ref.k_ref.v_ref, bf16[1024,768]{1,0:T(8,128)(2,1)} %shard_map.78.q_ref.k_ref.v_ref, bf16[1024,768]{1,0:T(8,128)(2,1)} %shard_map.78.q_ref.k_ref.v_ref, bf16[64,1280]{1,0:T(8,128)(2,1)} %copy-done.3, ...), custom_call_target="tpu_custom_call" | custom-call | flops 536870912 | bytes 2097152 | tf_op jit(solution)/shard_map/pallas_call | solution.py:235
  198.1 14.0 %collective-permute-done.41 = bf16[2,18,5,256]{3,2,1,0:T(8,128)(2,1)S(1)} collective-permute-done((bf16[2,18,5,256]{3,2,1,0:T(8,128)(2,1)S(1)}, bf16[2,18,5,256]{3,2,1,0:T(8,128)(2,1)S(1)}, u32[]{:S(2)}, u32[]{:S(2)}) %collective-permute-start.41) | collective-permute-done | bytes 92192 | tf_op jit(solution)/shard_map/ppermute | solution.py:21
  213.0 11.3 %collective-permute-done.19.refs_7_ = bf16[480,1152]{1,0:T(8,128)(2,1)} collective-permute-done((bf16[480,1152]{1,0:T(8,128)(2,1)}, bf16[480,1152]{1,0:T(8,128)(2,1)}, u32[]{:S(2)}, u32[]{:S(2)}) %collective-permute-start.19) | collective-permute-done | bytes 1105952 | tf_op jit(solution)/shard_map/ppermute | solution.py:21
  224.3 14.2 %shard_map.75.q_ref.k_ref.v_ref = bf16[1024,1152]{1,0:T(8,128)(2,1)} custom-call(s32[3]{0:T(128)} %pad_add_fusion.1.place, bf16[1024,2560]{1,0:T(8,128)(2,1)} %bitcast.54, bf16[160,1152]{1,0:T(8,128)(2,1)} %copy-done.12, bf16[480,1152]{1,0:T(8,128)(2,1)} %pad_maximum_fusion.refs_1_, bf16[160,1152]{1,0:T(8,128)(2,1)} %copy-done.30, ...), custom_call_target="tpu_custom_call" | custom-call | flops 6039797760 | bytes 5898240 | tf_op jit(solution)/shard_map/pallas_call | solution.py:142
  238.5 5.8 %shard_map.77 = bf16[1024,384]{1,0:T(8,128)(2,1)} custom-call(s32[3]{0:T(128)} %pad_add_fusion.info, bf16[1024,1152]{1,0:T(8,128)(2,1)} %shard_map.75.q_ref.k_ref.v_ref, bf16[1024,1152]{1,0:T(8,128)(2,1)} %shard_map.75.q_ref.k_ref.v_ref, bf16[1024,1152]{1,0:T(8,128)(2,1)} %shard_map.75.q_ref.k_ref.v_ref, bf16[64,1280]{1,0:T(8,128)(2,1)} %copy-done.3, ...), custom_call_target="tpu_custom_call" | custom-call | flops 805306368 | bytes 3145728 | tf_op jit(solution)/shard_map/pallas_call | solution.py:235
  249.3 3.3 %collective-permute-done.25 = bf16[2,5,32,384]{3,2,1,0:T(8,128)(2,1)S(1)} collective-permute-done((bf16[2,5,32,384]{3,2,1,0:T(8,128)(2,1)S(1)}, bf16[2,5,32,384]{3,2,1,0:T(8,128)(2,1)S(1)}, u32[]{:S(2)}, u32[]{:S(2)}) %collective-permute-start.25) | collective-permute-done | bytes 245792 | tf_op jit(solution)/shard_map/ppermute | solution.py:21
  252.5 5.8 %collective-permute-done.26 = bf16[2,5,32,384]{3,2,1,0:T(8,128)(2,1)S(1)} collective-permute-done((bf16[2,5,32,384]{3,2,1,0:T(8,128)(2,1)S(1)}, bf16[2,5,32,384]{3,2,1,0:T(8,128)(2,1)S(1)}, u32[]{:S(2)}, u32[]{:S(2)}) %collective-permute-start.26) | collective-permute-done | bytes 245792 | tf_op jit(solution)/shard_map/ppermute | solution.py:21
  260.5 4.3 %collective-permute-done.27 = bf16[2,18,5,384]{3,2,1,0:T(8,128)(2,1)S(1)} collective-permute-done((bf16[2,18,5,384]{3,2,1,0:T(8,128)(2,1)S(1)}, bf16[2,18,5,384]{3,2,1,0:T(8,128)(2,1)S(1)}, u32[]{:S(2)}, u32[]{:S(2)}) %collective-permute-start.27) | collective-permute-done | bytes 138272 | tf_op jit(solution)/shard_map/ppermute | solution.py:21
  (203 shorter events, 80.4 us)
Async XLA Ops:
  2.0 78.8 %collective-permute-start = (s32[1]{0:T(128)}, s32[1]{0:T(128)}, u32[]{:S(2)}, u32[]{:S(2)}) collective-permute-start(s32[1]{0:T(128)} %bitcast.3), channel_id=1, source_target_pairs={{0,1},{1,0},{2,3},{3,2},{4,5},{5,4},{6,7},{7,6},{8,9},{9,8},{10,11... | collective-permute-start | bytes 20 | tf_op jit(solution)/shard_map/ppermute | solution.py:21
  5.0 32.0 %collective-permute-start.2 = (bf16[160,1152]{1,0:T(8,128)(2,1)S(1)}, bf16[160,1152]{1,0:T(8,128)(2,1)S(1)}, u32[]{:S(2)}, u32[]{:S(2)}) collective-permute-start(bf16[160,1152]{1,0:T(8,128)(2,1)S(1)} %slice.257.refs_0_), channel_id=1, source_target_pairs={{0,8},{4,12},{8,0},{12,4},{1,9},{5,13},{9,1},{13,5},{2,10},{6,14},... | collective-permute-start | bytes 1105928 | tf_op jit(solution)/shard_map/ppermute | solution.py:67
  12.0 23.6 %collective-permute-start.28 = (bf16[160,768]{1,0:T(8,128)(2,1)}, bf16[160,768]{1,0:T(8,128)(2,1)}, u32[]{:S(2)}, u32[]{:S(2)}) collective-permute-start(bf16[160,768]{1,0:T(8,128)(2,1)} %slice.301.refs_0_), channel_id=1, source_target_pairs={{0,8},{4,12},{8,0},{12,4},{1,9},{5,13},{9,1},{13,5},{2,10},{6,14},... | collective-permute-start | bytes 737288 | tf_op jit(solution)/shard_map/ppermute | solution.py:67
  13.8 27.0 %collective-permute-start.30 = (bf16[160,768]{1,0:T(8,128)(2,1)}, bf16[160,768]{1,0:T(8,128)(2,1)S(1)}, u32[]{:S(2)}, u32[]{:S(2)}) collective-permute-start(bf16[160,768]{1,0:T(8,128)(2,1)} %slice.301.refs_0_), channel_id=1, source_target_pairs={{0,4},{4,8},{8,12},{1,5},{5,9},{9,13},{2,6},{6,10},{10,14},{3,7},{... | collective-permute-start | bytes 737288 | tf_op jit(solution)/shard_map/ppermute | solution.py:67
  17.1 28.6 %collective-permute-start.31 = (bf16[160,768]{1,0:T(8,128)(2,1)}, bf16[160,768]{1,0:T(8,128)(2,1)S(1)}, u32[]{:S(2)}, u32[]{:S(2)}) collective-permute-start(bf16[160,768]{1,0:T(8,128)(2,1)} %slice.301.refs_0_), channel_id=1, source_target_pairs={{4,0},{8,4},{12,8},{5,1},{9,5},{13,9},{6,2},{10,6},{14,10},{7,3},{... | collective-permute-start | bytes 737288 | tf_op jit(solution)/shard_map/ppermute | solution.py:67
  35.6 21.5 %collective-permute-start.29 = (bf16[160,768]{1,0:T(8,128)(2,1)}, bf16[160,768]{1,0:T(8,128)(2,1)S(1)}, u32[]{:S(2)}, u32[]{:S(2)}) collective-permute-start(bf16[160,768]{1,0:T(8,128)(2,1)} %collective-permute-done.28), channel_id=1, source_target_pairs={{4,0},{8,12},{5,1},{9,13},{6,2},{10,14},{7,3},{11,15},{20,16},{24,... | collective-permute-start | bytes 737288 | tf_op jit(solution)/shard_map/ppermute | solution.py:68
  37.8 21.3 %collective-permute-start.3 = (bf16[2,4,16,2560]{3,2,1,0:T(8,128)(2,1)S(1)}, bf16[2,4,16,2560]{3,2,1,0:T(8,128)(2,1)S(1)}, u32[]{:S(2)}, u32[]{:S(2)}) collective-permute-start(bf16[2,4,16,2560]{3,2,1,0:T(8,128)(2,1)S(1)} %pad_maximum_fusion.4), channel_id=1, source_target_pairs={{0,4},{4,8},{8,12},{12,0},{1,5},{5,9},{9,13},{13,1},{2,6},{6,10},{... | collective-permute-start | bytes 1966088 | tf_op jit(solution)/shard_map/ppermute | solution.py:21
  40.9 45.4 %collective-permute-start.12 = (bf16[160,1152]{1,0:T(8,128)(2,1)S(1)}, bf16[160,1152]{1,0:T(8,128)(2,1)S(1)}, u32[]{:S(2)}, u32[]{:S(2)}) collective-permute-start(bf16[160,1152]{1,0:T(8,128)(2,1)S(1)} %copy-done.13), channel_id=1, source_target_pairs={{0,4},{4,8},{8,12},{1,5},{5,9},{9,13},{2,6},{6,10},{10,14},{3,7},{... | collective-permute-start | bytes 1105928 | tf_op jit(solution)/shard_map/ppermute | solution.py:67
  45.7 41.9 %collective-permute-start.13 = (bf16[160,1152]{1,0:T(8,128)(2,1)S(1)}, bf16[160,1152]{1,0:T(8,128)(2,1)S(1)}, u32[]{:S(2)}, u32[]{:S(2)}) collective-permute-start(bf16[160,1152]{1,0:T(8,128)(2,1)S(1)} %copy-done.13), channel_id=1, source_target_pairs={{4,0},{8,4},{12,8},{5,1},{9,5},{13,9},{6,2},{10,6},{14,10},{7,3},{... | collective-permute-start | bytes 1105928 | tf_op jit(solution)/shard_map/ppermute | solution.py:67
  57.2 28.1 %collective-permute-start.32 = (bf16[160,768]{1,0:T(8,128)(2,1)S(1)}, bf16[160,768]{1,0:T(8,128)(2,1)}, u32[]{:S(2)}, u32[]{:S(2)}) collective-permute-start(bf16[160,768]{1,0:T(8,128)(2,1)S(1)} %copy-done.21), channel_id=1, source_target_pairs={{0,16},{16,0},{1,17},{17,1},{2,18},{18,2},{3,19},{19,3},{4,20},{20... | collective-permute-start | bytes 737288 | tf_op jit(solution)/shard_map/ppermute | solution.py:21
  59.1 20.6 %collective-permute-start.4 = (bf16[2,4,16,2560]{3,2,1,0:T(8,128)(2,1)S(1)}, bf16[2,4,16,2560]{3,2,1,0:T(8,128)(2,1)S(1)}, u32[]{:S(2)}, u32[]{:S(2)}) collective-permute-start(bf16[2,4,16,2560]{3,2,1,0:T(8,128)(2,1)S(1)} %pad_maximum_fusion.5), channel_id=1, source_target_pairs={{0,12},{4,0},{8,4},{12,8},{1,13},{5,1},{9,5},{13,9},{2,14},{6,2},{... | collective-permute-start | bytes 1966088 | tf_op jit(solution)/shard_map/ppermute | solution.py:21
  80.8 23.5 %collective-permute-start.33 = (bf16[480,768]{1,0:T(8,128)(2,1)}, bf16[480,768]{1,0:T(8,128)(2,1)}, u32[]{:S(2)}, u32[]{:S(2)}) collective-permute-start(bf16[480,768]{1,0:T(8,128)(2,1)} %pad_maximum_fusion.3.refs_1_), channel_id=1, source_target_pairs={{0,16},{16,0},{1,17},{17,1},{2,18},{18,2},{3,19},{19,3},{4,20},{20... | collective-permute-start | bytes 2211848 | tf_op jit(solution)/shard_map/ppermute | solution.py:21
  83.0 22.1 %collective-permute-start.35 = (bf16[480,768]{1,0:T(8,128)(2,1)}, bf16[480,768]{1,0:T(8,128)(2,1)}, u32[]{:S(2)}, u32[]{:S(2)}) collective-permute-start(bf16[480,768]{1,0:T(8,128)(2,1)} %pad_maximum_fusion.3.refs_1_), channel_id=1, source_target_pairs={{0,2},{2,0},{1,3},{3,1},{4,6},{6,4},{5,7},{7,5},{8,10},{10,8},{9,1... | collective-permute-start | bytes 2211848 | tf_op jit(solution)/shard_map/ppermute | solution.py:21
  85.3 26.9 %collective-permute-start.5 = (bf16[2,16,4,2560]{3,2,1,0:T(4,128)(2,1)}, bf16[2,16,4,2560]{3,2,1,0:T(4,128)(2,1)}, u32[]{:S(2)}, u32[]{:S(2)}) collective-permute-start(bf16[2,16,4,2560]{3,2,1,0:T(4,128)(2,1)} %fusion.26), channel_id=1, source_target_pairs={{0,2},{2,0},{1,3},{3,1},{4,6},{6,4},{5,7},{7,5},{8,10},{10,8},{9,1... | collective-permute-start | bytes 1966088 | tf_op jit(solution)/shard_map/ppermute | solution.py:21
  87.6 31.2 %collective-permute-start.7 = (bf16[16,16,2560]{2,1,0:T(8,128)(2,1)S(1)}, bf16[16,16,2560]{2,1,0:T(8,128)(2,1)}, u32[]{:S(2)}, u32[]{:S(2)}) collective-permute-start(bf16[16,16,2560]{2,1,0:T(8,128)(2,1)S(1)} %bitcast.62), channel_id=1, source_target_pairs={{0,1},{1,0},{2,3},{3,2},{4,5},{5,4},{6,7},{7,6},{8,9},{9,8},{10,11... | collective-permute-start | bytes 3932168 | tf_op jit(solution)/shard_map/ppermute | solution.py:21
  95.0 28.1 %collective-permute-start.8 = (bf16[16,16,2560]{2,1,0:T(8,128)(2,1)S(1)}, bf16[16,16,2560]{2,1,0:T(8,128)(2,1)}, u32[]{:S(2)}, u32[]{:S(2)}) collective-permute-start(bf16[16,16,2560]{2,1,0:T(8,128)(2,1)S(1)} %bitcast.58), channel_id=1, source_target_pairs={{0,1},{1,0},{2,3},{3,2},{4,5},{5,4},{6,7},{7,6},{8,9},{9,8},{10,11... | collective-permute-start | bytes 3932168 | tf_op jit(solution)/shard_map/ppermute | solution.py:21
  118.8 57.9 %collective-permute-start.17 = (bf16[480,1152]{1,0:T(8,128)(2,1)}, bf16[480,1152]{1,0:T(8,128)(2,1)}, u32[]{:S(2)}, u32[]{:S(2)}) collective-permute-start(bf16[480,1152]{1,0:T(8,128)(2,1)} %pad_maximum_fusion.refs_1_), channel_id=1, source_target_pairs={{0,2},{2,0},{1,3},{3,1},{4,6},{6,4},{5,7},{7,5},{8,10},{10,8},{9,1... | collective-permute-start | bytes 3317768 | tf_op jit(solution)/shard_map/ppermute | solution.py:21
  123.1 27.1 %collective-permute-start.34 = (bf16[160,768]{1,0:T(8,128)(2,1)S(1)}, bf16[160,768]{1,0:T(8,128)(2,1)S(1)}, u32[]{:S(2)}, u32[]{:S(2)}) collective-permute-start(bf16[160,768]{1,0:T(8,128)(2,1)S(1)} %copy-done.21), channel_id=1, source_target_pairs={{0,2},{2,0},{1,3},{3,1},{4,6},{6,4},{5,7},{7,5},{8,10},{10,8},{9,1... | collective-permute-start | bytes 737288 | tf_op jit(solution)/shard_map/ppermute | solution.py:21
  123.6 31.9 %collective-permute-start.36 = (bf16[160,768]{1,0:T(8,128)(2,1)}, bf16[160,768]{1,0:T(8,128)(2,1)S(1)}, u32[]{:S(2)}, u32[]{:S(2)}) collective-permute-start(bf16[160,768]{1,0:T(8,128)(2,1)} %collective-permute-done.32.refs_2_), channel_id=1, source_target_pairs={{0,2},{2,0},{1,3},{3,1},{4,6},{6,4},{5,7},{7,5},{8,10},{10,8},{9,1... | collective-permute-start | bytes 737288 | tf_op jit(solution)/shard_map/ppermute | solution.py:21
  124.6 38.8 %collective-permute-start.37 = (bf16[240,768]{1,0:T(8,128)(2,1)S(1)}, bf16[240,768]{1,0:T(8,128)(2,1)S(1)}, u32[]{:S(2)}, u32[]{:S(2)}) collective-permute-start(bf16[240,768]{1,0:T(8,128)(2,1)S(1)} %slice.359), channel_id=1, source_target_pairs={{0,2},{2,0},{1,3},{3,1},{4,6},{6,4},{5,7},{7,5},{8,10},{10,8},{9,1... | collective-permute-start | bytes 1105928 | tf_op jit(solution)/shard_map/ppermute | solution.py:21
  125.1 38.3 %collective-permute-start.38 = (bf16[240,768]{1,0:T(8,128)(2,1)S(1)}, bf16[240,768]{1,0:T(8,128)(2,1)S(1)}, u32[]{:S(2)}, u32[]{:S(2)}) collective-permute-start(bf16[240,768]{1,0:T(8,128)(2,1)S(1)} %slice.360), channel_id=1, source_target_pairs={{0,16},{16,0},{1,17},{17,1},{2,18},{18,2},{3,19},{19,3},{4,20},{20... | collective-permute-start | bytes 1105928 | tf_op jit(solution)/shard_map/ppermute | solution.py:21
  150.2 43.0 %collective-permute-start.14 = (bf16[160,1152]{1,0:T(8,128)(2,1)S(1)}, bf16[160,1152]{1,0:T(8,128)(2,1)S(1)}, u32[]{:S(2)}, u32[]{:S(2)}) collective-permute-start(bf16[160,1152]{1,0:T(8,128)(2,1)S(1)} %copy-done.14), channel_id=1, source_target_pairs={{0,16},{16,0},{1,17},{17,1},{2,18},{18,2},{3,19},{19,3},{4,20},{20... | collective-permute-start | bytes 1105928 | tf_op jit(solution)/shard_map/ppermute | solution.py:21
  175.7 36.5 %collective-permute-start.15 = (bf16[480,1152]{1,0:T(8,128)(2,1)}, bf16[480,1152]{1,0:T(8,128)(2,1)S(1)}, u32[]{:S(2)}, u32[]{:S(2)}) collective-permute-start(bf16[480,1152]{1,0:T(8,128)(2,1)} %pad_maximum_fusion.refs_1_), channel_id=1, source_target_pairs={{0,16},{16,0},{1,17},{17,1},{2,18},{18,2},{3,19},{19,3},{4,20},{20... | collective-permute-start | bytes 3317768 | tf_op jit(solution)/shard_map/ppermute | solution.py:21
  176.7 47.6 %collective-permute-start.19 = (bf16[480,1152]{1,0:T(8,128)(2,1)}, bf16[480,1152]{1,0:T(8,128)(2,1)}, u32[]{:S(2)}, u32[]{:S(2)}) collective-permute-start(bf16[480,1152]{1,0:T(8,128)(2,1)} %collective-permute-done.17.refs_5_), channel_id=1, source_target_pairs={{0,16},{16,0},{1,17},{17,1},{2,18},{18,2},{3,19},{19,3},{4,20},{20... | collective-permute-start | bytes 3317768 | tf_op jit(solution)/shard_map/ppermute | solution.py:21
  (57 other events, 692.8 us)
where the time goes:
time: 278 us; the launch traced here: 276 us
  waiting for transfers between devices  125 us (45%)
  starting transfers between devices  62.8 us (23%)
  Pallas kernels  45.9 us (17%)
  other arithmetic  24 us (9%)
  local copies, waits for them, and re-layouts  11.5 us (4%)
  between operations  7.48 us (3%)
    ppermute x36, waiting for transfers between devices, cyc(): lax.ppermute(x, axis, [(i, (i + step) % count) for i in range(count)])  95.1 us
    ppermute x36, starting transfers between devices, cyc(): lax.ppermute(x, axis, [(i, (i + step) % count) for i in range(count)])  46.1 us
    pallas_call x2, Pallas kernels, project(): pl.pallas_call(functools.partial(project_kernel, pieces=tuple(pieces), si...  25 us
    ppermute x6, waiting for transfers between devices, along_line(): got[d] = lax.ppermute(block, axis, pairs)  16.5 us
    ppermute x6, starting transfers between devices, along_line(): got[d] = lax.ppermute(block, axis, pairs)  14.1 us
    ppermute x2, waiting for transfers between devices, along_line(): passed = lax.ppermute(got[2], axis, [(1, 0), (2, 3)])  13.2 us
    pallas_call x2, Pallas kernels, attend(): pl.pallas_call(functools.partial(attend_kernel, width=width), grid_spec=p...  10.5 us
    pallas_call x1, Pallas kernels, shifted_tokens(): pl.pallas_call(rows_kernel, in_specs=[pl.BlockSpec(memory_space=pltpu.SME...  6.94 us
  transfers between devices with their start and end apart: 44, of which 16 were waited for; matrix products, arithmetic and copies ran while one was open for 9% of the time, Pallas kernels for 9%

commit v1 on v0

--- a/solution.py
+++ b/solution.py
@@ -27,9 +27,10 @@
     return jnp.concatenate([first, second], axis=axis)
 
 
-def halves_kernel(core_ref, w_ref, mine_ref, other_ref, *, heads, chunks):
+def halves_kernel(w_ref, mine_ref, other_ref, *, heads, chunks):
     half = heads // 2
-    for ref, core in ((mine_ref, core_ref[0]), (other_ref, 1 - core_ref[0])):
+    own = lax.axis_index("core")
+    for ref, core in ((mine_ref, own), (other_ref, 1 - own)):
         first, at = 0, 0
         for count in chunks:
             for kind in range(ref.shape[1] // (half * HD)):
@@ -42,17 +43,13 @@
 def core_halves(block, heads, chunks):
     rows, cols = block.shape
     half = jax.ShapeDtypeStruct((rows, cols // 2), block.dtype)
-    core = lax.axis_index("core").reshape(1)
     return pl.pallas_call(
         functools.partial(halves_kernel, heads=heads, chunks=chunks),
-        in_specs=[
-            pl.BlockSpec(memory_space=pltpu.SMEM),
-            pl.BlockSpec(memory_space=pltpu.VMEM),
-        ],
+        in_specs=[pl.BlockSpec(memory_space=pltpu.VMEM)],
         out_specs=[pl.BlockSpec(memory_space=pltpu.VMEM)] * 2,
         out_shape=[half, half],
         cost_estimate=pl.CostEstimate(flops=0, transcendentals=0, bytes_accessed=4 * block.size),
-    )(core, block)
+    )(block)
 
 
 def along_line(block, axis):
@@ -107,8 +104,9 @@
     return arrays, pieces, side, early
 
 
-def project_kernel(place, tok_ref, *refs, pieces, side, has):
-    arrays, (out_ref, full, sems) = refs[:-3], refs[-3:]
+def project_kernel(tok_ref, *refs, pieces, side, has):
+    arrays, (out_ref, full, held, made, sems, tok_sems, out_sems) = refs[:-7], refs[-7:]
+    place = [lax.axis_index(axis) for axis in ("clip", "ha", "wy")]
     copies = []
     for k, (array, begin, count, other_clip, d, other_wy, skip) in enumerate(pieces):
         clip = 1 - place[0] if other_clip else place[0]
@@ -120,41 +118,61 @@
                 arrays[array].at[pl.ds(begin, count)], full.at[pl.ds(at, count)], sems.at[k]
             )
         )
+    high = held.shape[1]
+    tiles = held.shape[0]
+    loads = [
+        pltpu.make_async_copy(tok_ref.at[pl.ds(k * high, high)], held.at[k], tok_sems.at[k])
+        for k in range(tiles)
+    ]
+    stores = [
+        pltpu.make_async_copy(made.at[k], out_ref.at[pl.ds(k * high, high)], out_sems.at[k])
+        for k in range(tiles)
+    ]
     for copy in copies:
         copy.start()
+    loads[0].start()
     for copy in copies:
         copy.wait()
-
-    @pl.loop(0, tok_ref.shape[0] // 256)
-    def _(step):
-        rows = pl.ds(pl.multiple_of(step * 256, 256), 256)
-        out_ref[rows, :] = jnp.dot(
-            tok_ref[rows, :], full[...], preferred_element_type=jnp.float32
-        ).astype(out_ref.dtype)
-
-
-def project(place, tokens, arrays, pieces, side):
+    for k in range(tiles):
+        loads[k].wait()
+        if k == 0:
+            for load in loads[1:]:
+                load.start()
+        made[k] = jnp.dot(held[k], full[...], preferred_element_type=jnp.float32).astype(
+            made.dtype
+        )
+        stores[k].start()
+    for store in stores:
+        store.wait()
+
+
+def project(tokens, arrays, pieces, side):
     rows, width = tokens.shape
     cols = arrays[0].shape[1]
     if pieces is None:
         return jnp.dot(tokens, arrays[0], preferred_element_type=jnp.float32).astype(tokens.dtype)
-    vmem = pl.BlockSpec(memory_space=pltpu.VMEM)
+    hbm = pl.BlockSpec(memory_space=pl.ANY)
+    tiles = 4
     return pl.pallas_call(
         functools.partial(
             project_kernel, pieces=tuple(pieces), side=side, has=lax.axis_size("ha")
         ),
-        in_specs=[pl.BlockSpec(memory_space=pltpu.SMEM), vmem]
-        + [pl.BlockSpec(memory_space=pl.ANY)] * len(arrays),
-        out_specs=vmem,
+        in_specs=[hbm]
+        + [hbm] * len(arrays),
+        out_specs=hbm,
         out_shape=jax.ShapeDtypeStruct((rows, cols), jnp.bfloat16),
         scratch_shapes=[
             pltpu.VMEM((width, cols), jnp.bfloat16),
+            pltpu.VMEM((tiles, rows // tiles, width), jnp.bfloat16),
+            pltpu.VMEM((tiles, rows // tiles, cols), jnp.bfloat16),
             pltpu.SemaphoreType.DMA((len(pieces),)),
+            pltpu.SemaphoreType.DMA((tiles,)),
+            pltpu.SemaphoreType.DMA((tiles,)),
         ],
         cost_estimate=pl.CostEstimate(
             flops=2 * rows * width * cols, transcendentals=0, bytes_accessed=2 * width * cols
         ),
-    )(place, tokens, *arrays)
+    )(tokens, *arrays)
 
 
 def gathered_pairs(pairs, heads):
@@ -167,14 +185,17 @@
     return [both] + [cyc(both, "ha", d) for d in range(1, lax.axis_size("ha"))]
 
 
-def attend_kernel(info, q_ref, k_ref, v_ref, *refs, width):
+def attend_kernel(shifts_ref, own_ref, twin_ref, q_ref, k_ref, v_ref, *refs, width):
     far_refs, (out_ref, bias_ref) = refs[:-2], refs[-2:]
     count = len(far_refs) // 2
     far_keys = jnp.concatenate([ref[...] for ref in far_refs[:count]], axis=0)
     far_values = jnp.concatenate([ref[...] for ref in far_refs[count:]], axis=0)
     rate = math.log2(math.e) / math.sqrt(HD)
     tokens = bias_ref.shape[0]
-    shift = info[0]
+    shift = shifts_ref[0, 1]
+    first_core = lax.axis_index("core") == 0
+    low = jnp.where(first_core, own_ref[0, 0], twin_ref[0, 0])
+    high = jnp.where(first_core, twin_ref[0, 0], own_ref[0, 0])
 
     def window(shape, axis):
         slot = lax.broadcasted_iota(jnp.int32, shape, axis) & (width - 1)
@@ -211,7 +232,7 @@
             mixed = mixed + weighted(jnp.exp2((far - top) * rate), far_values)
         result = mixed[:, :HD] / mixed[:, HD:]
         if part >= 2:
-            keep = jnp.where(window((tokens, 1), 0) < width // 16, info[1], info[2]) > 0
+            keep = jnp.where(window((tokens, 1), 0) < width // 16, low, high) > 0
             result = jnp.where(keep, result, 0.0)
         out_ref[rows, :] = result.astype(out_ref.dtype)
 
@@ -223,10 +244,10 @@
     far_rows = sum(part.shape[0] for part in far)
 
     def near_spec(offset):
-        return pl.BlockSpec((total, HD), lambda i, s: (0, offset + i))
+        return pl.BlockSpec((total, HD), lambda i, *s: (0, offset + i))
 
     def far_specs(offset):
-        def at(i, s):
+        def at(i, *s):
             return 0, offset + first + i
 
         return [pl.BlockSpec((part.shape[0], HD), at) for part in far]
@@ -235,7 +256,7 @@
     return pl.pallas_call(
         functools.partial(attend_kernel, width=width),
         grid_spec=pltpu.PrefetchScalarGridSpec(
-            num_scalar_prefetch=1,
+            num_scalar_prefetch=3,
             grid=(count,),
             in_specs=[
                 near_spec(0),
@@ -244,7 +265,7 @@
             ]
             + far_specs(0)
             + far_specs(all_heads),
-            out_specs=pl.BlockSpec((total, HD), lambda i, s: (0, i)),
+            out_specs=pl.BlockSpec((total, HD), lambda i, *s: (0, i)),
             scratch_shapes=[pltpu.VMEM((tokens, tokens), jnp.float32)],
         ),
         out_shape=jax.ShapeDtypeStruct((total, count * HD), jnp.bfloat16),
@@ -253,11 +274,12 @@
             transcendentals=2 * count * tokens * keys,
             bytes_accessed=8 * total * count * HD,
         ),
-    )(info, projected, projected, projected, *far, *far)
-
-
-def rows_kernel(info, mine_ref, other_ref, *refs):
-    halves, (out_ref, sems) = (refs[:4], refs[4:8]), refs[8:]
+    )(*info, projected, projected, projected, *far, *far)
+
+
+def rows_kernel(shifts_ref, mine_ref, other_ref, *refs):
+    halves, (out_ref, sems) = (refs[:4], refs[4:8]), refs[-2:]
+    info = shifts_ref[0, 0], lax.axis_index("core"), shifts_ref[0, 1]
     rows, cols = refs[0].shape[:2]
     rim = refs[2].shape[1]
 
@@ -306,10 +328,11 @@
             out_ref[branch, row, place] = jnp.where(taken, both, held).astype(out_ref.dtype)
 
 
-def shifted_tokens(lat_cond, lat_uncond, shift_rows, shift_cols, after):
+def shifted_tokens(lat_cond, lat_uncond, shifts, after, taps):
     core = lax.axis_index("core")
     rows, cols, width = lat_cond.shape
     pair = [lat_cond, lat_uncond]
+    shift_rows = shifts[0, 0]
     late = list(lax.optimization_barrier((lat_cond, lat_uncond, after))[:2])
     twin = [cyc(lat_cond, "core", 1), cyc(lat_uncond, "core", 1)]
     above = cyc(jnp.stack([x[rows - RIM :] for x in late]), "ha", 1)
@@ -321,21 +344,22 @@
     high += [above[:, :, cols - RIM :], below[:, :, cols - RIM :]]
     own, up, dn = (jnp.where(core == 0, a, b) for a, b in zip(low, high))
     tall = jnp.concatenate([up, own, dn], axis=1)
-    edge = lax.dynamic_slice_in_dim(tall, RIM + shift_rows, rows, axis=1)
+    start = (RIM + shift_rows).astype(jnp.uint32)
+    edge = lax.dynamic_slice_in_dim(tall, start, rows, axis=1)
     mine = cyc(edge, "wy", 1)
     other = cyc(mine, "core", 1)
     return pl.pallas_call(
         rows_kernel,
         in_specs=[pl.BlockSpec(memory_space=pltpu.SMEM)]
         + [pl.BlockSpec(memory_space=pltpu.VMEM)] * 2
-        + [pl.BlockSpec(memory_space=pl.ANY)] * len(halves),
+        + [pl.BlockSpec(memory_space=pl.ANY)] * (len(halves) + len(taps)),
         out_specs=pl.BlockSpec(memory_space=pltpu.VMEM),
         out_shape=jax.ShapeDtypeStruct((2, rows, 2 * cols, width), lat_cond.dtype),
         scratch_shapes=[pltpu.SemaphoreType.DMA((rows, 4))],
         cost_estimate=pl.CostEstimate(
             flops=0, transcendentals=0, bytes_accessed=16 * rows * cols * width
         ),
-    )(jnp.stack([shift_rows, core, shift_cols]), mine, other, *halves)
+    )(shifts, mine, other, *halves, *taps)
 
 
 def refined_part(attended, taps, shift_rows, shift_cols):
@@ -344,7 +368,8 @@
     above = cyc(attended[:, rows - rim :], "ha", 1)
     below = cyc(attended[:, :rim], "ha", -1)
     tall = jnp.concatenate([above, attended, below], axis=1)
-    tall = lax.dynamic_slice_in_dim(tall, RIM - shift_rows, rows + 2, axis=1)
+    start = (RIM - shift_rows).astype(jnp.uint32)
+    tall = lax.dynamic_slice_in_dim(tall, start, rows + 2, axis=1)
     ha, wy = lax.axis_index("ha"), lax.axis_index("wy")
     row = lax.broadcasted_iota(jnp.int32, (1, rows + 2, 1, 1), 1)
     inside = ((row > 0) | (ha > 0)) & ((row < rows + 1) | (ha < lax.axis_size("ha") - 1))
@@ -381,10 +406,7 @@
     heads = qkv_weight.shape[1] // (3 * HD)
     core = lax.axis_index("core")
     shift_rows, shift_cols = shifts[0, 0], shifts[0, 1]
-    own_flag = guide_mask[0]
-    flags = ordered(core, own_flag, cyc(own_flag, "core", 1), 0)
-    info = jnp.concatenate([shifts[0, 1:], flags])
-    place = jnp.stack([lax.axis_index(a) for a in ("clip", "ha", "wy")])
+    info = shifts, guide_mask, cyc(guide_mask, "core", 1)
     mine, other = core_halves(qkv_weight, heads, CHUNKS)
     block = ordered(core, mine, cyc(other, "core", 1), 0)
     chips = (lax.axis_size("clip"), lax.axis_size("wy"))
@@ -396,20 +418,21 @@
     for tag, first, count in zip(tags, firsts, CHUNKS):
         columns = block[:, 3 * first * HD : 3 * (first + count) * HD]
         weights.append(weight_pieces(columns, tag, chips))
+    taps = []
+    for first, count in zip(firsts, CHUNKS):
+        at = ((core * (heads // 2) + first) * HD).astype(jnp.uint32)
+        taps.append(lax.dynamic_slice_in_dim(kernel, at, count * HD, axis=2))
     tokens = shifted_tokens(
-        latent_cond[0, 0], latent_uncond[0, 0], shift_rows, shift_cols, weights[0][3]
+        latent_cond[0, 0], latent_uncond[0, 0], shifts, weights[0][3], taps
     )
     tokens = tokens.reshape(-1, width_d)
     far = gathered_pairs(cond_pairs[0], heads)
     parts, others = [], []
-    for tag, first, count, weight in zip(tags, firsts, CHUNKS, weights):
-        projected = project(place, tokens, *weight[:3])
+    for tag, first, count, weight, part_taps in zip(tags, firsts, CHUNKS, weights, taps):
+        projected = project(tokens, *weight[:3])
         attended = attend(info, projected, far, first, count, 2 * cols)
         attended = attended.reshape(2, rows, 2 * cols, count * HD)
-        taps = lax.dynamic_slice_in_dim(
-            kernel, (core * (heads // 2) + first) * HD, count * HD, axis=2
-        )
-        part = refined_part(attended, taps, shift_rows, shift_cols)
+        part = refined_part(attended, part_taps, shift_rows, shift_cols)
         low, high = part[:, :, :cols], part[:, :, cols:]
         parts.append(jnp.where(core == 0, low, high))
         others.append(cyc(jnp.where(core == 0, high, low), "core", 1))

time: 278 us -> 283 us (1.018)
  waiting for transfers between devices: 125 us -> 133 us
  local copies, waits for them, and re-layouts: 11.5 us -> 16.3 us
  other arithmetic: 24 us -> 20.4 us
    ppermute x2, waiting for transfers between devices: 13.2 us -> 20.2 us  [along_line(): passed = lax.ppermute(got[2], axis, [(1, 0), (2, 3)])]
    pallas_call x2, Pallas kernels: 25 us -> 21.4 us  [project(): pl.pallas_call(functools.partial(project_kernel, pieces=tuple(pieces), si...]
    ppermute x36, waiting for transfers between devices: 95.1 us -> 98.5 us  [cyc(): lax.ppermute(x, axis, [(i, (i + step) % count) for i in range(count)])]
    dynamic_slice x0 -> x2, local copies, waits for them, and re-layouts: none -> 2.84 us  [on_device(): taps.append(lax.dynamic_slice_in_dim(kernel, at, count * HD, axis=2))]
  transfers between devices with their start and end apart: 44 -> 44, of which waited for: 16 -> 15; matrix products, arithmetic and copies ran while one was open for 9% -> 9% of each run, Pallas kernels for 9% -> 8%
where the time goes in v1:
time: 283 us; the launch traced here: 282 us
  waiting for transfers between devices  133 us (47%)
  starting transfers between devices  63.3 us (22%)
  Pallas kernels  43.5 us (15%)
  other arithmetic  20.4 us (7%)
  local copies, waits for them, and re-layouts  16.3 us (6%)
  between operations  5.34 us (2%)
    ppermute x36, waiting for transfers between devices, cyc(): lax.ppermute(x, axis, [(i, (i + step) % count) for i in range(count)])  98.5 us
    ppermute x36, starting transfers between devices, cyc(): lax.ppermute(x, axis, [(i, (i + step) % count) for i in range(count)])  48.3 us
    pallas_call x2, Pallas kernels, project(): pl.pallas_call(functools.partial(project_kernel, pieces=tuple(pieces), si...  21.4 us
    ppermute x2, waiting for transfers between devices, along_line(): passed = lax.ppermute(got[2], axis, [(1, 0), (2, 3)])  20.2 us
    ppermute x6, waiting for transfers between devices, along_line(): got[d] = lax.ppermute(block, axis, pairs)  14.5 us
    ppermute x6, starting transfers between devices, along_line(): got[d] = lax.ppermute(block, axis, pairs)  12.5 us
    pallas_call x2, Pallas kernels, attend(): pl.pallas_call(functools.partial(attend_kernel, width=width), grid_spec=p...  11.6 us
    pallas_call x1, Pallas kernels, shifted_tokens(): pl.pallas_call(rows_kernel, in_specs=[pl.BlockSpec(memory_space=pltpu.SME...  6.93 us
  transfers between devices with their start and end apart: 44, of which 15 were waited for; matrix products, arithmetic and copies ran while one was open for 9% of the time, Pallas kernels for 8%

profile of v1, /device:TPU:1, one launch (start us, length us, event | category | flops | bytes accessed | tf_op | source)
XLA Modules:
  0.0 282.0 jit_solution(11608492486852082469)
XLA Ops:
  5.7 3.4 %collective-permute-start.2 = (bf16[160,1152]{1,0:T(8,128)(2,1)}, bf16[160,1152]{1,0:T(8,128)(2,1)S(1)}, u32[]{:S(2)}, u32[]{:S(2)}) collective-permute-start(bf16[160,1152]{1,0:T(8,128)(2,1)} %slice.256.refs_0_), channel_id=1, source_target_pairs={{0,8},{4,12},{8,0},{12,4},{1,9},{5,13},{9,1},{13,5},{2,10},{6,14},... | collective-permute-start | bytes 1105928 | tf_op jit(solution)/shard_map/ppermute | solution.py:64
  13.4 3.3 %collective-permute-start.12 = (bf16[160,1152]{1,0:T(8,128)(2,1)}, bf16[160,1152]{1,0:T(8,128)(2,1)S(1)}, u32[]{:S(2)}, u32[]{:S(2)}) collective-permute-start(bf16[160,1152]{1,0:T(8,128)(2,1)} %slice.256.refs_0_), channel_id=1, source_target_pairs={{0,4},{4,8},{8,12},{1,5},{5,9},{9,13},{2,6},{6,10},{10,14},{3,7},{... | collective-permute-start | bytes 1105928 | tf_op jit(solution)/shard_map/ppermute | solution.py:64
  21.9 14.5 %collective-permute-done.28 = bf16[160,768]{1,0:T(8,128)(2,1)} collective-permute-done((bf16[160,768]{1,0:T(8,128)(2,1)S(1)}, bf16[160,768]{1,0:T(8,128)(2,1)}, u32[]{:S(2)}, u32[]{:S(2)}) %collective-permute-start.28) | collective-permute-done | bytes 245792 | tf_op jit(solution)/shard_map/ppermute | solution.py:64
  44.0 15.5 %collective-permute-done.29 = bf16[160,768]{1,0:T(8,128)(2,1)S(1)} collective-permute-done((bf16[160,768]{1,0:T(8,128)(2,1)}, bf16[160,768]{1,0:T(8,128)(2,1)S(1)}, u32[]{:S(2)}, u32[]{:S(2)}) %collective-permute-start.29) | collective-permute-done | bytes 245792 | tf_op jit(solution)/shard_map/ppermute | solution.py:65
  62.5 3.9 %collective-permute-start.4 = (bf16[2,4,16,2560]{3,2,1,0:T(8,128)(2,1)S(1)}, bf16[2,4,16,2560]{3,2,1,0:T(8,128)(2,1)S(1)}, u32[]{:S(2)}, u32[]{:S(2)}) collective-permute-start(bf16[2,4,16,2560]{3,2,1,0:T(8,128)(2,1)S(1)} %pad_maximum_fusion.5), channel_id=1, source_target_pairs={{0,12},{4,0},{8,4},{12,8},{1,13},{5,1},{9,5},{13,9},{2,14},{6,2},{... | collective-permute-start | bytes 1966088 | tf_op jit(solution)/shard_map/ppermute | solution.py:21
  66.5 15.0 %collective-permute-done.4.refs_3_ = bf16[2,4,16,2560]{3,2,1,0:T(8,128)(2,1)S(1)} collective-permute-done((bf16[2,4,16,2560]{3,2,1,0:T(8,128)(2,1)S(1)}, bf16[2,4,16,2560]{3,2,1,0:T(8,128)(2,1)S(1)}, u32[]{:S(2)}, u32[]{:S(2)}) %collective-permute-start.4) | collective-permute-done | bytes 655392 | tf_op jit(solution)/shard_map/ppermute | solution.py:21
  90.3 4.7 %collective-permute-done.11 = bf16[160,1152]{1,0:T(8,128)(2,1)S(1)} collective-permute-done((bf16[160,1152]{1,0:T(8,128)(2,1)S(1)}, bf16[160,1152]{1,0:T(8,128)(2,1)S(1)}, u32[]{:S(2)}, u32[]{:S(2)}) %collective-permute-start.11) | collective-permute-done | bytes 368672 | tf_op jit(solution)/shard_map/ppermute | solution.py:65
  95.8 3.8 %collective-permute-start.8 = (bf16[16,16,2560]{2,1,0:T(8,128)(2,1)S(1)}, bf16[16,16,2560]{2,1,0:T(8,128)(2,1)}, u32[]{:S(2)}, u32[]{:S(2)}) collective-permute-start(bf16[16,16,2560]{2,1,0:T(8,128)(2,1)S(1)} %bitcast.46), channel_id=1, source_target_pairs={{0,1},{1,0},{2,3},{3,2},{4,5},{5,4},{6,7},{7,6},{8,9},{9,8},{10,11... | collective-permute-start | bytes 3932168 | tf_op jit(solution)/shard_map/ppermute | solution.py:21
  101.1 3.8 %collective-permute-start.10 = (bf16[2,4,16,2560]{3,2,1,0:T(8,128)(2,1)}, bf16[2,4,16,2560]{3,2,1,0:T(8,128)(2,1)}, u32[]{:S(2)}, u32[]{:S(2)}) collective-permute-start(bf16[2,4,16,2560]{3,2,1,0:T(8,128)(2,1)} %copy-done.8), channel_id=1, source_target_pairs={{0,1},{1,0},{2,3},{3,2},{4,5},{5,4},{6,7},{7,6},{8,9},{9,8},{10,11... | collective-permute-start | bytes 1966088 | tf_op jit(solution)/shard_map/ppermute | solution.py:21
  104.8 7.8 %collective-permute-done.5.mine_ref = bf16[2,16,4,2560]{3,2,1,0:T(4,128)(2,1)} collective-permute-done((bf16[2,16,4,2560]{3,2,1,0:T(4,128)(2,1)}, bf16[2,16,4,2560]{3,2,1,0:T(4,128)(2,1)}, u32[]{:S(2)}, u32[]{:S(2)}) %collective-permute-start.5) | collective-permute-done | bytes 655392 | tf_op jit(solution)/shard_map/ppermute | solution.py:21
  112.6 3.3 %collective-permute-start.6 = (bf16[2,16,4,2560]{3,2,1,0:T(4,128)(2,1)}, bf16[2,16,4,2560]{3,2,1,0:T(4,128)(2,1)}, u32[]{:S(2)}, u32[]{:S(2)}) collective-permute-start(bf16[2,16,4,2560]{3,2,1,0:T(4,128)(2,1)} %collective-permute-done.5.mine_ref), channel_id=1, source_target_pairs={{0,1},{1,0},{2,3},{3,2},{4,5},{5,4},{6,7},{7,6},{8,9},{9,8},{10,11... | collective-permute-start | bytes 1966088 | tf_op jit(solution)/shard_map/ppermute | solution.py:21
  128.7 6.9 %shard_map.74 = bf16[2,16,32,2560]{3,2,1,0:T(8,128)(2,1)} custom-call(s32[1,2]{1,0:T(1,128)} %shifts_ref.5, bf16[2,16,4,2560]{3,2,1,0:T(4,128)(2,1)} %collective-permute-done.5.mine_ref, bf16[2,16,4,2560]{3,2,1,0:T(4,128)(2,1)} %collective-permute-done.6.other_ref, bf16[16,16,2560]{2,1,0:T(8,128)(2,1)} %bitcast.47, bf16[16,16,2560]{2,1,0:T(8,128)(2,1)} %bitcast.43, ...), custom_call_target="tpu_custom_call" | custom-call | bytes 10485760 | tf_op jit(solution)/shard_map/pallas_call | solution.py:351
  135.6 14.0 %collective-permute-done.34.refs_4_ = bf16[160,768]{1,0:T(8,128)(2,1)S(1)} collective-permute-done((bf16[160,768]{1,0:T(8,128)(2,1)S(1)}, bf16[160,768]{1,0:T(8,128)(2,1)S(1)}, u32[]{:S(2)}, u32[]{:S(2)}) %collective-permute-start.34) | collective-permute-done | bytes 245792 | tf_op jit(solution)/shard_map/ppermute | solution.py:21
  151.0 3.9 %collective-permute-done.36.refs_6_ = bf16[160,768]{1,0:T(8,128)(2,1)S(1)} collective-permute-done((bf16[160,768]{1,0:T(8,128)(2,1)}, bf16[160,768]{1,0:T(8,128)(2,1)S(1)}, u32[]{:S(2)}, u32[]{:S(2)}) %collective-permute-start.36) | collective-permute-done | bytes 245792 | tf_op jit(solution)/shard_map/ppermute | solution.py:21
  154.9 7.9 %collective-permute-done.37.refs_7_ = bf16[240,768]{1,0:T(8,128)(2,1)S(1)} collective-permute-done((bf16[240,768]{1,0:T(8,128)(2,1)S(1)}, bf16[240,768]{1,0:T(8,128)(2,1)S(1)}, u32[]{:S(2)}, u32[]{:S(2)}) %collective-permute-start.37) | collective-permute-done | bytes 368672 | tf_op jit(solution)/shard_map/ppermute | solution.py:21
  165.1 9.7 %shard_map.78.q_ref.k_ref.v_ref = bf16[1024,768]{1,0:T(8,128)(2,1)} custom-call(bf16[1024,2560]{1,0:T(8,128)(2,1)} %bitcast.41, bf16[160,768]{1,0:T(8,128)(2,1)} %copy-done.15, bf16[480,768]{1,0:T(8,128)(2,1)} %pad_maximum_fusion.3.refs_1_, bf16[160,768]{1,0:T(8,128)(2,1)} %copy-done.26, bf16[480,768]{1,0:T(8,128)(2,1)} %collective-permute-done.33.refs_3_, ...), custom_call_target="tpu_custom_call" | custom-call | flops 4026531840 | bytes 3932160 | tf_op jit(solution)/shard_map/pallas_call | solution.py:156
  178.7 5.2 %shard_map.79 = bf16[1024,256]{1,0:T(8,128)(2,1)} custom-call(s32[1,2]{1,0:T(1,128)} %shifts_ref.5, s32[1,1]{1,0:T(1,128)S(6)} %copy.11.own_ref, s32[1,1]{1,0:T(1,128)} %collective-permute-done.twin_ref, bf16[1024,768]{1,0:T(8,128)(2,1)} %shard_map.78.q_ref.k_ref.v_ref, bf16[1024,768]{1,0:T(8,128)(2,1)} %shard_map.78.q_ref.k_ref.v_ref, ...), custom_call_target="tpu_custom_call" | custom-call | flops 536870912 | bytes 2097152 | tf_op jit(solution)/shard_map/pallas_call | solution.py:256
  199.0 13.4 %collective-permute-done.41 = bf16[2,18,5,256]{3,2,1,0:T(8,128)(2,1)S(1)} collective-permute-done((bf16[2,18,5,256]{3,2,1,0:T(8,128)(2,1)S(1)}, bf16[2,18,5,256]{3,2,1,0:T(8,128)(2,1)S(1)}, u32[]{:S(2)}, u32[]{:S(2)}) %collective-permute-start.41) | collective-permute-done | bytes 92192 | tf_op jit(solution)/shard_map/ppermute | solution.py:21
  212.5 18.8 %collective-permute-done.19.refs_7_ = bf16[480,1152]{1,0:T(8,128)(2,1)} collective-permute-done((bf16[480,1152]{1,0:T(8,128)(2,1)}, bf16[480,1152]{1,0:T(8,128)(2,1)}, u32[]{:S(2)}, u32[]{:S(2)}) %collective-permute-start.19) | collective-permute-done | bytes 1105952 | tf_op jit(solution)/shard_map/ppermute | solution.py:21
  231.4 11.6 %shard_map.75.q_ref.k_ref.v_ref = bf16[1024,1152]{1,0:T(8,128)(2,1)} custom-call(bf16[1024,2560]{1,0:T(8,128)(2,1)} %bitcast.42, bf16[160,1152]{1,0:T(8,128)(2,1)} %slice.256.refs_0_, bf16[480,1152]{1,0:T(8,128)(2,1)} %pad_maximum_fusion.refs_1_, bf16[160,1152]{1,0:T(8,128)(2,1)} %copy-done.21, bf16[480,1152]{1,0:T(8,128)(2,1)} %copy-done.20, ...), custom_call_target="tpu_custom_call" | custom-call | flops 6039797760 | bytes 5898240 | tf_op jit(solution)/shard_map/pallas_call | solution.py:156
  243.0 6.4 %shard_map.77 = bf16[1024,384]{1,0:T(8,128)(2,1)} custom-call(s32[1,2]{1,0:T(1,128)} %shifts_ref.5, s32[1,1]{1,0:T(1,128)S(6)} %copy.11.own_ref, s32[1,1]{1,0:T(1,128)} %collective-permute-done.twin_ref, bf16[1024,1152]{1,0:T(8,128)(2,1)} %shard_map.75.q_ref.k_ref.v_ref, bf16[1024,1152]{1,0:T(8,128)(2,1)} %shard_map.75.q_ref.k_ref.v_ref, ...), custom_call_target="tpu_custom_call" | custom-call | flops 805306368 | bytes 3145728 | tf_op jit(solution)/shard_map/pallas_call | solution.py:256
  254.3 3.3 %collective-permute-done.25 = bf16[2,5,32,384]{3,2,1,0:T(8,128)(2,1)S(1)} collective-permute-done((bf16[2,5,32,384]{3,2,1,0:T(8,128)(2,1)S(1)}, bf16[2,5,32,384]{3,2,1,0:T(8,128)(2,1)S(1)}, u32[]{:S(2)}, u32[]{:S(2)}) %collective-permute-start.25) | collective-permute-done | bytes 245792 | tf_op jit(solution)/shard_map/ppermute | solution.py:21
  257.6 6.4 %collective-permute-done.26 = bf16[2,5,32,384]{3,2,1,0:T(8,128)(2,1)S(1)} collective-permute-done((bf16[2,5,32,384]{3,2,1,0:T(8,128)(2,1)S(1)}, bf16[2,5,32,384]{3,2,1,0:T(8,128)(2,1)S(1)}, u32[]{:S(2)}, u32[]{:S(2)}) %collective-permute-start.26) | collective-permute-done | bytes 245792 | tf_op jit(solution)/shard_map/ppermute | solution.py:21
  266.2 4.5 %collective-permute-done.27 = bf16[2,18,5,384]{3,2,1,0:T(8,128)(2,1)S(1)} collective-permute-done((bf16[2,18,5,384]{3,2,1,0:T(8,128)(2,1)S(1)}, bf16[2,18,5,384]{3,2,1,0:T(8,128)(2,1)S(1)}, u32[]{:S(2)}, u32[]{:S(2)}) %collective-permute-start.27) | collective-permute-done | bytes 138272 | tf_op jit(solution)/shard_map/ppermute | solution.py:21
  (186 shorter events, 85.4 us)
Async XLA Ops:
  5.7 32.1 %collective-permute-start.2 = (bf16[160,1152]{1,0:T(8,128)(2,1)}, bf16[160,1152]{1,0:T(8,128)(2,1)S(1)}, u32[]{:S(2)}, u32[]{:S(2)}) collective-permute-start(bf16[160,1152]{1,0:T(8,128)(2,1)} %slice.256.refs_0_), channel_id=1, source_target_pairs={{0,8},{4,12},{8,0},{12,4},{1,9},{5,13},{9,1},{13,5},{2,10},{6,14},... | collective-permute-start | bytes 1105928 | tf_op jit(solution)/shard_map/ppermute | solution.py:64
  12.0 24.4 %collective-permute-start.28 = (bf16[160,768]{1,0:T(8,128)(2,1)S(1)}, bf16[160,768]{1,0:T(8,128)(2,1)}, u32[]{:S(2)}, u32[]{:S(2)}) collective-permute-start(bf16[160,768]{1,0:T(8,128)(2,1)S(1)} %slice.301.refs_0_), channel_id=1, source_target_pairs={{0,8},{4,12},{8,0},{12,4},{1,9},{5,13},{9,1},{13,5},{2,10},{6,14},... | collective-permute-start | bytes 737288 | tf_op jit(solution)/shard_map/ppermute | solution.py:64
  13.4 72.6 %collective-permute-start.12 = (bf16[160,1152]{1,0:T(8,128)(2,1)}, bf16[160,1152]{1,0:T(8,128)(2,1)S(1)}, u32[]{:S(2)}, u32[]{:S(2)}) collective-permute-start(bf16[160,1152]{1,0:T(8,128)(2,1)} %slice.256.refs_0_), channel_id=1, source_target_pairs={{0,4},{4,8},{8,12},{1,5},{5,9},{9,13},{2,6},{6,10},{10,14},{3,7},{... | collective-permute-start | bytes 1105928 | tf_op jit(solution)/shard_map/ppermute | solution.py:64
  16.6 25.0 %collective-permute-start.30 = (bf16[160,768]{1,0:T(8,128)(2,1)S(1)}, bf16[160,768]{1,0:T(8,128)(2,1)S(1)}, u32[]{:S(2)}, u32[]{:S(2)}) collective-permute-start(bf16[160,768]{1,0:T(8,128)(2,1)S(1)} %slice.301.refs_0_), channel_id=1, source_target_pairs={{0,4},{4,8},{8,12},{1,5},{5,9},{9,13},{2,6},{6,10},{10,14},{3,7},{... | collective-permute-start | bytes 737288 | tf_op jit(solution)/shard_map/ppermute | solution.py:64
  19.9 23.1 %collective-permute-start.31 = (bf16[160,768]{1,0:T(8,128)(2,1)S(1)}, bf16[160,768]{1,0:T(8,128)(2,1)S(1)}, u32[]{:S(2)}, u32[]{:S(2)}) collective-permute-start(bf16[160,768]{1,0:T(8,128)(2,1)S(1)} %slice.301.refs_0_), channel_id=1, source_target_pairs={{4,0},{8,4},{12,8},{5,1},{9,5},{13,9},{6,2},{10,6},{14,10},{7,3},{... | collective-permute-start | bytes 737288 | tf_op jit(solution)/shard_map/ppermute | solution.py:64
  36.5 23.0 %collective-permute-start.29 = (bf16[160,768]{1,0:T(8,128)(2,1)}, bf16[160,768]{1,0:T(8,128)(2,1)S(1)}, u32[]{:S(2)}, u32[]{:S(2)}) collective-permute-start(bf16[160,768]{1,0:T(8,128)(2,1)} %collective-permute-done.28), channel_id=1, source_target_pairs={{4,0},{8,12},{5,1},{9,13},{6,2},{10,14},{7,3},{11,15},{20,16},{24,... | collective-permute-start | bytes 737288 | tf_op jit(solution)/shard_map/ppermute | solution.py:65
  38.6 23.9 %collective-permute-start.3 = (bf16[2,4,16,2560]{3,2,1,0:T(8,128)(2,1)S(1)}, bf16[2,4,16,2560]{3,2,1,0:T(8,128)(2,1)S(1)}, u32[]{:S(2)}, u32[]{:S(2)}) collective-permute-start(bf16[2,4,16,2560]{3,2,1,0:T(8,128)(2,1)S(1)} %pad_maximum_fusion.4), channel_id=1, source_target_pairs={{0,4},{4,8},{8,12},{12,0},{1,5},{5,9},{9,13},{13,1},{2,6},{6,10},{... | collective-permute-start | bytes 1966088 | tf_op jit(solution)/shard_map/ppermute | solution.py:21
  41.7 45.6 %collective-permute-start.13 = (bf16[160,1152]{1,0:T(8,128)(2,1)}, bf16[160,1152]{1,0:T(8,128)(2,1)S(1)}, u32[]{:S(2)}, u32[]{:S(2)}) collective-permute-start(bf16[160,1152]{1,0:T(8,128)(2,1)} %slice.256.refs_0_), channel_id=1, source_target_pairs={{4,0},{8,4},{12,8},{5,1},{9,5},{13,9},{6,2},{10,6},{14,10},{7,3},{... | collective-permute-start | bytes 1105928 | tf_op jit(solution)/shard_map/ppermute | solution.py:64
  43.0 42.7 %collective-permute-start.32 = (bf16[160,768]{1,0:T(8,128)(2,1)S(1)}, bf16[160,768]{1,0:T(8,128)(2,1)S(1)}, u32[]{:S(2)}, u32[]{:S(2)}) collective-permute-start(bf16[160,768]{1,0:T(8,128)(2,1)S(1)} %slice.301.refs_0_), channel_id=1, source_target_pairs={{0,16},{16,0},{1,17},{17,1},{2,18},{18,2},{3,19},{19,3},{4,20},{20... | collective-permute-start | bytes 737288 | tf_op jit(solution)/shard_map/ppermute | solution.py:21
  59.5 23.1 %collective-permute-start.21 = (bf16[32,1280]{1,0:T(8,128)(2,1)S(1)}, bf16[32,1280]{1,0:T(8,128)(2,1)S(1)}, u32[]{:S(2)}, u32[]{:S(2)}) collective-permute-start(bf16[32,1280]{1,0:T(8,128)(2,1)S(1)} %pad_maximum_fusion.11), channel_id=1, source_target_pairs={{0,2},{2,0},{1,3},{3,1},{4,6},{6,4},{5,7},{7,5},{8,10},{10,8},{9,1... | collective-permute-start | bytes 245768 | tf_op jit(solution)/shard_map/ppermute | solution.py:21
  85.7 26.9 %collective-permute-start.5 = (bf16[2,16,4,2560]{3,2,1,0:T(4,128)(2,1)}, bf16[2,16,4,2560]{3,2,1,0:T(4,128)(2,1)}, u32[]{:S(2)}, u32[]{:S(2)}) collective-permute-start(bf16[2,16,4,2560]{3,2,1,0:T(4,128)(2,1)} %fusion.26), channel_id=1, source_target_pairs={{0,2},{2,0},{1,3},{3,1},{4,6},{6,4},{5,7},{7,5},{8,10},{10,8},{9,1... | collective-permute-start | bytes 1966088 | tf_op jit(solution)/shard_map/ppermute | solution.py:21
  87.3 31.0 %collective-permute-start.7 = (bf16[16,16,2560]{2,1,0:T(8,128)(2,1)S(1)}, bf16[16,16,2560]{2,1,0:T(8,128)(2,1)}, u32[]{:S(2)}, u32[]{:S(2)}) collective-permute-start(bf16[16,16,2560]{2,1,0:T(8,128)(2,1)S(1)} %bitcast.50), channel_id=1, source_target_pairs={{0,1},{1,0},{2,3},{3,2},{4,5},{5,4},{6,7},{7,6},{8,9},{9,8},{10,11... | collective-permute-start | bytes 3932168 | tf_op jit(solution)/shard_map/ppermute | solution.py:21
  95.8 28.5 %collective-permute-start.8 = (bf16[16,16,2560]{2,1,0:T(8,128)(2,1)S(1)}, bf16[16,16,2560]{2,1,0:T(8,128)(2,1)}, u32[]{:S(2)}, u32[]{:S(2)}) collective-permute-start(bf16[16,16,2560]{2,1,0:T(8,128)(2,1)S(1)} %bitcast.46), channel_id=1, source_target_pairs={{0,1},{1,0},{2,3},{3,2},{4,5},{5,4},{6,7},{7,6},{8,9},{9,8},{10,11... | collective-permute-start | bytes 3932168 | tf_op jit(solution)/shard_map/ppermute | solution.py:21
  101.1 23.6 %collective-permute-start.9 = (bf16[2,4,16,2560]{3,2,1,0:T(8,128)(2,1)S(1)}, bf16[2,4,16,2560]{3,2,1,0:T(8,128)(2,1)}, u32[]{:S(2)}, u32[]{:S(2)}) collective-permute-start(bf16[2,4,16,2560]{3,2,1,0:T(8,128)(2,1)S(1)} %collective-permute-done.3.refs_2_), channel_id=1, source_target_pairs={{0,1},{1,0},{2,3},{3,2},{4,5},{5,4},{6,7},{7,6},{8,9},{9,8},{10,11... | collective-permute-start | bytes 1966088 | tf_op jit(solution)/shard_map/ppermute | solution.py:21
  101.1 24.8 %collective-permute-start.10 = (bf16[2,4,16,2560]{3,2,1,0:T(8,128)(2,1)}, bf16[2,4,16,2560]{3,2,1,0:T(8,128)(2,1)}, u32[]{:S(2)}, u32[]{:S(2)}) collective-permute-start(bf16[2,4,16,2560]{3,2,1,0:T(8,128)(2,1)} %copy-done.8), channel_id=1, source_target_pairs={{0,1},{1,0},{2,3},{3,2},{4,5},{5,4},{6,7},{7,6},{8,9},{9,8},{10,11... | collective-permute-start | bytes 1966088 | tf_op jit(solution)/shard_map/ppermute | solution.py:21
  118.2 58.2 %collective-permute-start.17 = (bf16[480,1152]{1,0:T(8,128)(2,1)}, bf16[480,1152]{1,0:T(8,128)(2,1)}, u32[]{:S(2)}, u32[]{:S(2)}) collective-permute-start(bf16[480,1152]{1,0:T(8,128)(2,1)} %pad_maximum_fusion.refs_1_), channel_id=1, source_target_pairs={{0,2},{2,0},{1,3},{3,1},{4,6},{6,4},{5,7},{7,5},{8,10},{10,8},{9,1... | collective-permute-start | bytes 3317768 | tf_op jit(solution)/shard_map/ppermute | solution.py:21
  124.3 25.3 %collective-permute-start.34 = (bf16[160,768]{1,0:T(8,128)(2,1)S(1)}, bf16[160,768]{1,0:T(8,128)(2,1)S(1)}, u32[]{:S(2)}, u32[]{:S(2)}) collective-permute-start(bf16[160,768]{1,0:T(8,128)(2,1)S(1)} %slice.301.refs_0_), channel_id=1, source_target_pairs={{0,2},{2,0},{1,3},{3,1},{4,6},{6,4},{5,7},{7,5},{8,10},{10,8},{9,1... | collective-permute-start | bytes 737288 | tf_op jit(solution)/shard_map/ppermute | solution.py:21
  124.6 30.3 %collective-permute-start.36 = (bf16[160,768]{1,0:T(8,128)(2,1)}, bf16[160,768]{1,0:T(8,128)(2,1)S(1)}, u32[]{:S(2)}, u32[]{:S(2)}) collective-permute-start(bf16[160,768]{1,0:T(8,128)(2,1)} %copy-done.26), channel_id=1, source_target_pairs={{0,2},{2,0},{1,3},{3,1},{4,6},{6,4},{5,7},{7,5},{8,10},{10,8},{9,1... | collective-permute-start | bytes 737288 | tf_op jit(solution)/shard_map/ppermute | solution.py:21
  125.9 36.9 %collective-permute-start.37 = (bf16[240,768]{1,0:T(8,128)(2,1)S(1)}, bf16[240,768]{1,0:T(8,128)(2,1)S(1)}, u32[]{:S(2)}, u32[]{:S(2)}) collective-permute-start(bf16[240,768]{1,0:T(8,128)(2,1)S(1)} %slice.359), channel_id=1, source_target_pairs={{0,2},{2,0},{1,3},{3,1},{4,6},{6,4},{5,7},{7,5},{8,10},{10,8},{9,1... | collective-permute-start | bytes 1105928 | tf_op jit(solution)/shard_map/ppermute | solution.py:21
  126.1 37.8 %collective-permute-start.38 = (bf16[240,768]{1,0:T(8,128)(2,1)S(1)}, bf16[240,768]{1,0:T(8,128)(2,1)S(1)}, u32[]{:S(2)}, u32[]{:S(2)}) collective-permute-start(bf16[240,768]{1,0:T(8,128)(2,1)S(1)} %slice.360), channel_id=1, source_target_pairs={{0,16},{16,0},{1,17},{17,1},{2,18},{18,2},{3,19},{19,3},{4,20},{20... | collective-permute-start | bytes 1105928 | tf_op jit(solution)/shard_map/ppermute | solution.py:21
  149.6 25.2 %collective-permute-start = (s32[1,1]{1,0:T(1,128)}, s32[1,1]{1,0:T(1,128)}, u32[]{:S(2)}, u32[]{:S(2)}) collective-permute-start(s32[1,1]{1,0:T(1,128)} %param.11), channel_id=1, source_target_pairs={{0,1},{1,0},{2,3},{3,2},{4,5},{5,4},{6,7},{7,6},{8,9},{9,8},{10,11... | collective-permute-start | bytes 20 | tf_op jit(solution)/shard_map/ppermute | solution.py:21
  154.9 20.9 %collective-permute-start.22 = (bf16[64,1280]{1,0:T(8,128)(2,1)S(1)}, bf16[64,1280]{1,0:T(8,128)(2,1)S(1)}, u32[]{:S(2)}, u32[]{:S(2)}) collective-permute-start(bf16[64,1280]{1,0:T(8,128)(2,1)S(1)} %constant_dynamic-update-slice_fusion.refs_0_.refs_4_), channel_id=1, source_target_pairs={{0,4},{4,8},{8,12},{12,0},{1,5},{5,9},{9,13},{13,1},{2,6},{6,10},{... | collective-permute-start | bytes 491528 | tf_op jit(solution)/shard_map/ppermute | solution.py:21
  175.8 36.7 %collective-permute-start.15 = (bf16[480,1152]{1,0:T(8,128)(2,1)}, bf16[480,1152]{1,0:T(8,128)(2,1)S(1)}, u32[]{:S(2)}, u32[]{:S(2)}) collective-permute-start(bf16[480,1152]{1,0:T(8,128)(2,1)} %pad_maximum_fusion.refs_1_), channel_id=1, source_target_pairs={{0,16},{16,0},{1,17},{17,1},{2,18},{18,2},{3,19},{19,3},{4,20},{20... | collective-permute-start | bytes 3317768 | tf_op jit(solution)/shard_map/ppermute | solution.py:21
  176.4 55.0 %collective-permute-start.19 = (bf16[480,1152]{1,0:T(8,128)(2,1)}, bf16[480,1152]{1,0:T(8,128)(2,1)}, u32[]{:S(2)}, u32[]{:S(2)}) collective-permute-start(bf16[480,1152]{1,0:T(8,128)(2,1)} %collective-permute-done.17.refs_5_), channel_id=1, source_target_pairs={{0,16},{16,0},{1,17},{17,1},{2,18},{18,2},{3,19},{19,3},{4,20},{20... | collective-permute-start | bytes 3317768 | tf_op jit(solution)/shard_map/ppermute | solution.py:21
  (49 other events, 764.2 us)

commit v2 on v1

--- a/solution.py
+++ b/solution.py
@@ -223,13 +223,12 @@
         rows = slice(part * tokens, (part + 1) * tokens)
         q = q_ref[rows, :]
         near = product(q, k_ref[rows, :]) + bias_ref[...]
+        values = v_ref[rows, :]
+        if part < 2:
+            near = jnp.concatenate([near, product(q, far_keys)], axis=1)
+            values = jnp.concatenate([values, far_values], axis=0)
         top = jnp.max(near, axis=-1, keepdims=True)
-        if part < 2:
-            far = product(q, far_keys)
-            top = jnp.maximum(top, jnp.max(far, axis=-1, keepdims=True))
-        mixed = weighted(jnp.exp2((near - top) * rate), v_ref[rows, :])
-        if part < 2:
-            mixed = mixed + weighted(jnp.exp2((far - top) * rate), far_values)
+        mixed = weighted(jnp.exp2((near - top) * rate), values)
         result = mixed[:, :HD] / mixed[:, HD:]
         if part >= 2:
             keep = jnp.where(window((tokens, 1), 0) < width // 16, low, high) > 0

time: 283 us -> 283 us (level)
  no operation moved by 1% of the time
where the time goes in v2:
time: 283 us; the launch traced here: 282 us
  waiting for transfers between devices  133 us (47%)
  starting transfers between devices  63.3 us (22%)
  Pallas kernels  43.4 us (15%)
  other arithmetic  20.4 us (7%)
  local copies, waits for them, and re-layouts  16.3 us (6%)
  between operations  5.34 us (2%)
    ppermute x36, waiting for transfers between devices, cyc(): lax.ppermute(x, axis, [(i, (i + step) % count) for i in range(count)])  98.5 us
    ppermute x36, starting transfers between devices, cyc(): lax.ppermute(x, axis, [(i, (i + step) % count) for i in range(count)])  48.3 us
    pallas_call x2, Pallas kernels, project(): pl.pallas_call(functools.partial(project_kernel, pieces=tuple(pieces), si...  21.4 us
    ppermute x2, waiting for transfers between devices, along_line(): passed = lax.ppermute(got[2], axis, [(1, 0), (2, 3)])  20.2 us
    ppermute x6, waiting for transfers between devices, along_line(): got[d] = lax.ppermute(block, axis, pairs)  14.5 us
    ppermute x6, starting transfers between devices, along_line(): got[d] = lax.ppermute(block, axis, pairs)  12.5 us
    pallas_call x2, Pallas kernels, attend(): pl.pallas_call(functools.partial(attend_kernel, width=width), grid_spec=p...  11.6 us
    pallas_call x1, Pallas kernels, shifted_tokens(): pl.pallas_call(rows_kernel, in_specs=[pl.BlockSpec(memory_space=pltpu.SME...  6.93 us
  transfers between devices with their start and end apart: 44, of which 15 were waited for; matrix products, arithmetic and copies ran while one was open for 9% of the time, Pallas kernels for 8%

profile of v2, /device:TPU:1, one launch (start us, length us, event | category | flops | bytes accessed | tf_op | source)
XLA Modules:
  0.0 282.0 jit_solution(9000468752113670030)
XLA Ops:
  5.7 3.4 %collective-permute-start.2 = (bf16[160,1152]{1,0:T(8,128)(2,1)}, bf16[160,1152]{1,0:T(8,128)(2,1)S(1)}, u32[]{:S(2)}, u32[]{:S(2)}) collective-permute-start(bf16[160,1152]{1,0:T(8,128)(2,1)} %slice.256.refs_0_), channel_id=1, source_target_pairs={{0,8},{4,12},{8,0},{12,4},{1,9},{5,13},{9,1},{13,5},{2,10},{6,14},... | collective-permute-start | bytes 1105928 | tf_op jit(solution)/shard_map/ppermute | solution.py:64
  13.4 3.3 %collective-permute-start.12 = (bf16[160,1152]{1,0:T(8,128)(2,1)}, bf16[160,1152]{1,0:T(8,128)(2,1)S(1)}, u32[]{:S(2)}, u32[]{:S(2)}) collective-permute-start(bf16[160,1152]{1,0:T(8,128)(2,1)} %slice.256.refs_0_), channel_id=1, source_target_pairs={{0,4},{4,8},{8,12},{1,5},{5,9},{9,13},{2,6},{6,10},{10,14},{3,7},{... | collective-permute-start | bytes 1105928 | tf_op jit(solution)/shard_map/ppermute | solution.py:64
  21.9 14.5 %collective-permute-done.28 = bf16[160,768]{1,0:T(8,128)(2,1)} collective-permute-done((bf16[160,768]{1,0:T(8,128)(2,1)S(1)}, bf16[160,768]{1,0:T(8,128)(2,1)}, u32[]{:S(2)}, u32[]{:S(2)}) %collective-permute-start.28) | collective-permute-done | bytes 245792 | tf_op jit(solution)/shard_map/ppermute | solution.py:64
  44.0 15.5 %collective-permute-done.29 = bf16[160,768]{1,0:T(8,128)(2,1)S(1)} collective-permute-done((bf16[160,768]{1,0:T(8,128)(2,1)}, bf16[160,768]{1,0:T(8,128)(2,1)S(1)}, u32[]{:S(2)}, u32[]{:S(2)}) %collective-permute-start.29) | collective-permute-done | bytes 245792 | tf_op jit(solution)/shard_map/ppermute | solution.py:65
  62.5 3.9 %collective-permute-start.4 = (bf16[2,4,16,2560]{3,2,1,0:T(8,128)(2,1)S(1)}, bf16[2,4,16,2560]{3,2,1,0:T(8,128)(2,1)S(1)}, u32[]{:S(2)}, u32[]{:S(2)}) collective-permute-start(bf16[2,4,16,2560]{3,2,1,0:T(8,128)(2,1)S(1)} %pad_maximum_fusion.5), channel_id=1, source_target_pairs={{0,12},{4,0},{8,4},{12,8},{1,13},{5,1},{9,5},{13,9},{2,14},{6,2},{... | collective-permute-start | bytes 1966088 | tf_op jit(solution)/shard_map/ppermute | solution.py:21
  66.5 15.0 %collective-permute-done.4.refs_3_ = bf16[2,4,16,2560]{3,2,1,0:T(8,128)(2,1)S(1)} collective-permute-done((bf16[2,4,16,2560]{3,2,1,0:T(8,128)(2,1)S(1)}, bf16[2,4,16,2560]{3,2,1,0:T(8,128)(2,1)S(1)}, u32[]{:S(2)}, u32[]{:S(2)}) %collective-permute-start.4) | collective-permute-done | bytes 655392 | tf_op jit(solution)/shard_map/ppermute | solution.py:21
  90.3 4.7 %collective-permute-done.11 = bf16[160,1152]{1,0:T(8,128)(2,1)S(1)} collective-permute-done((bf16[160,1152]{1,0:T(8,128)(2,1)S(1)}, bf16[160,1152]{1,0:T(8,128)(2,1)S(1)}, u32[]{:S(2)}, u32[]{:S(2)}) %collective-permute-start.11) | collective-permute-done | bytes 368672 | tf_op jit(solution)/shard_map/ppermute | solution.py:65
  95.8 3.8 %collective-permute-start.8 = (bf16[16,16,2560]{2,1,0:T(8,128)(2,1)S(1)}, bf16[16,16,2560]{2,1,0:T(8,128)(2,1)}, u32[]{:S(2)}, u32[]{:S(2)}) collective-permute-start(bf16[16,16,2560]{2,1,0:T(8,128)(2,1)S(1)} %bitcast.46), channel_id=1, source_target_pairs={{0,1},{1,0},{2,3},{3,2},{4,5},{5,4},{6,7},{7,6},{8,9},{9,8},{10,11... | collective-permute-start | bytes 3932168 | tf_op jit(solution)/shard_map/ppermute | solution.py:21
  101.1 3.8 %collective-permute-start.10 = (bf16[2,4,16,2560]{3,2,1,0:T(8,128)(2,1)}, bf16[2,4,16,2560]{3,2,1,0:T(8,128)(2,1)}, u32[]{:S(2)}, u32[]{:S(2)}) collective-permute-start(bf16[2,4,16,2560]{3,2,1,0:T(8,128)(2,1)} %copy-done.8), channel_id=1, source_target_pairs={{0,1},{1,0},{2,3},{3,2},{4,5},{5,4},{6,7},{7,6},{8,9},{9,8},{10,11... | collective-permute-start | bytes 1966088 | tf_op jit(solution)/shard_map/ppermute | solution.py:21
  104.8 7.8 %collective-permute-done.5.mine_ref = bf16[2,16,4,2560]{3,2,1,0:T(4,128)(2,1)} collective-permute-done((bf16[2,16,4,2560]{3,2,1,0:T(4,128)(2,1)}, bf16[2,16,4,2560]{3,2,1,0:T(4,128)(2,1)}, u32[]{:S(2)}, u32[]{:S(2)}) %collective-permute-start.5) | collective-permute-done | bytes 655392 | tf_op jit(solution)/shard_map/ppermute | solution.py:21
  112.6 3.3 %collective-permute-start.6 = (bf16[2,16,4,2560]{3,2,1,0:T(4,128)(2,1)}, bf16[2,16,4,2560]{3,2,1,0:T(4,128)(2,1)}, u32[]{:S(2)}, u32[]{:S(2)}) collective-permute-start(bf16[2,16,4,2560]{3,2,1,0:T(4,128)(2,1)} %collective-permute-done.5.mine_ref), channel_id=1, source_target_pairs={{0,1},{1,0},{2,3},{3,2},{4,5},{5,4},{6,7},{7,6},{8,9},{9,8},{10,11... | collective-permute-start | bytes 1966088 | tf_op jit(solution)/shard_map/ppermute | solution.py:21
  128.7 6.9 %shard_map.74 = bf16[2,16,32,2560]{3,2,1,0:T(8,128)(2,1)} custom-call(s32[1,2]{1,0:T(1,128)} %shifts_ref.5, bf16[2,16,4,2560]{3,2,1,0:T(4,128)(2,1)} %collective-permute-done.5.mine_ref, bf16[2,16,4,2560]{3,2,1,0:T(4,128)(2,1)} %collective-permute-done.6.other_ref, bf16[16,16,2560]{2,1,0:T(8,128)(2,1)} %bitcast.47, bf16[16,16,2560]{2,1,0:T(8,128)(2,1)} %bitcast.43, ...), custom_call_target="tpu_custom_call" | custom-call | bytes 10485760 | tf_op jit(solution)/shard_map/pallas_call | solution.py:350
  135.6 14.0 %collective-permute-done.34.refs_4_ = bf16[160,768]{1,0:T(8,128)(2,1)S(1)} collective-permute-done((bf16[160,768]{1,0:T(8,128)(2,1)S(1)}, bf16[160,768]{1,0:T(8,128)(2,1)S(1)}, u32[]{:S(2)}, u32[]{:S(2)}) %collective-permute-start.34) | collective-permute-done | bytes 245792 | tf_op jit(solution)/shard_map/ppermute | solution.py:21
  151.0 3.9 %collective-permute-done.36.refs_6_ = bf16[160,768]{1,0:T(8,128)(2,1)S(1)} collective-permute-done((bf16[160,768]{1,0:T(8,128)(2,1)}, bf16[160,768]{1,0:T(8,128)(2,1)S(1)}, u32[]{:S(2)}, u32[]{:S(2)}) %collective-permute-start.36) | collective-permute-done | bytes 245792 | tf_op jit(solution)/shard_map/ppermute | solution.py:21
  154.9 7.9 %collective-permute-done.37.refs_7_ = bf16[240,768]{1,0:T(8,128)(2,1)S(1)} collective-permute-done((bf16[240,768]{1,0:T(8,128)(2,1)S(1)}, bf16[240,768]{1,0:T(8,128)(2,1)S(1)}, u32[]{:S(2)}, u32[]{:S(2)}) %collective-permute-start.37) | collective-permute-done | bytes 368672 | tf_op jit(solution)/shard_map/ppermute | solution.py:21
  165.1 9.7 %shard_map.78.q_ref.k_ref.v_ref = bf16[1024,768]{1,0:T(8,128)(2,1)} custom-call(bf16[1024,2560]{1,0:T(8,128)(2,1)} %bitcast.41, bf16[160,768]{1,0:T(8,128)(2,1)} %copy-done.15, bf16[480,768]{1,0:T(8,128)(2,1)} %pad_maximum_fusion.3.refs_1_, bf16[160,768]{1,0:T(8,128)(2,1)} %copy-done.26, bf16[480,768]{1,0:T(8,128)(2,1)} %collective-permute-done.33.refs_3_, ...), custom_call_target="tpu_custom_call" | custom-call | flops 4026531840 | bytes 3932160 | tf_op jit(solution)/shard_map/pallas_call | solution.py:156
  178.7 5.2 %shard_map.79 = bf16[1024,256]{1,0:T(8,128)(2,1)} custom-call(s32[1,2]{1,0:T(1,128)} %shifts_ref.5, s32[1,1]{1,0:T(1,128)S(6)} %copy.11.own_ref, s32[1,1]{1,0:T(1,128)} %collective-permute-done.twin_ref, bf16[1024,768]{1,0:T(8,128)(2,1)} %shard_map.78.q_ref.k_ref.v_ref, bf16[1024,768]{1,0:T(8,128)(2,1)} %shard_map.78.q_ref.k_ref.v_ref, ...), custom_call_target="tpu_custom_call" | custom-call | flops 536870912 | bytes 2097152 | tf_op jit(solution)/shard_map/pallas_call | solution.py:255
  199.0 13.4 %collective-permute-done.41 = bf16[2,18,5,256]{3,2,1,0:T(8,128)(2,1)S(1)} collective-permute-done((bf16[2,18,5,256]{3,2,1,0:T(8,128)(2,1)S(1)}, bf16[2,18,5,256]{3,2,1,0:T(8,128)(2,1)S(1)}, u32[]{:S(2)}, u32[]{:S(2)}) %collective-permute-start.41) | collective-permute-done | bytes 92192 | tf_op jit(solution)/shard_map/ppermute | solution.py:21
  212.5 18.9 %collective-permute-done.19.refs_7_ = bf16[480,1152]{1,0:T(8,128)(2,1)} collective-permute-done((bf16[480,1152]{1,0:T(8,128)(2,1)}, bf16[480,1152]{1,0:T(8,128)(2,1)}, u32[]{:S(2)}, u32[]{:S(2)}) %collective-permute-start.19) | collective-permute-done | bytes 1105952 | tf_op jit(solution)/shard_map/ppermute | solution.py:21
  231.4 11.6 %shard_map.75.q_ref.k_ref.v_ref = bf16[1024,1152]{1,0:T(8,128)(2,1)} custom-call(bf16[1024,2560]{1,0:T(8,128)(2,1)} %bitcast.42, bf16[160,1152]{1,0:T(8,128)(2,1)} %slice.256.refs_0_, bf16[480,1152]{1,0:T(8,128)(2,1)} %pad_maximum_fusion.refs_1_, bf16[160,1152]{1,0:T(8,128)(2,1)} %copy-done.21, bf16[480,1152]{1,0:T(8,128)(2,1)} %copy-done.20, ...), custom_call_target="tpu_custom_call" | custom-call | flops 6039797760 | bytes 5898240 | tf_op jit(solution)/shard_map/pallas_call | solution.py:156
  243.0 6.4 %shard_map.77 = bf16[1024,384]{1,0:T(8,128)(2,1)} custom-call(s32[1,2]{1,0:T(1,128)} %shifts_ref.5, s32[1,1]{1,0:T(1,128)S(6)} %copy.11.own_ref, s32[1,1]{1,0:T(1,128)} %collective-permute-done.twin_ref, bf16[1024,1152]{1,0:T(8,128)(2,1)} %shard_map.75.q_ref.k_ref.v_ref, bf16[1024,1152]{1,0:T(8,128)(2,1)} %shard_map.75.q_ref.k_ref.v_ref, ...), custom_call_target="tpu_custom_call" | custom-call | flops 805306368 | bytes 3145728 | tf_op jit(solution)/shard_map/pallas_call | solution.py:255
  254.3 3.3 %collective-permute-done.25 = bf16[2,5,32,384]{3,2,1,0:T(8,128)(2,1)S(1)} collective-permute-done((bf16[2,5,32,384]{3,2,1,0:T(8,128)(2,1)S(1)}, bf16[2,5,32,384]{3,2,1,0:T(8,128)(2,1)S(1)}, u32[]{:S(2)}, u32[]{:S(2)}) %collective-permute-start.25) | collective-permute-done | bytes 245792 | tf_op jit(solution)/shard_map/ppermute | solution.py:21
  257.6 6.4 %collective-permute-done.26 = bf16[2,5,32,384]{3,2,1,0:T(8,128)(2,1)S(1)} collective-permute-done((bf16[2,5,32,384]{3,2,1,0:T(8,128)(2,1)S(1)}, bf16[2,5,32,384]{3,2,1,0:T(8,128)(2,1)S(1)}, u32[]{:S(2)}, u32[]{:S(2)}) %collective-permute-start.26) | collective-permute-done | bytes 245792 | tf_op jit(solution)/shard_map/ppermute | solution.py:21
  266.2 4.5 %collective-permute-done.27 = bf16[2,18,5,384]{3,2,1,0:T(8,128)(2,1)S(1)} collective-permute-done((bf16[2,18,5,384]{3,2,1,0:T(8,128)(2,1)S(1)}, bf16[2,18,5,384]{3,2,1,0:T(8,128)(2,1)S(1)}, u32[]{:S(2)}, u32[]{:S(2)}) %collective-permute-start.27) | collective-permute-done | bytes 138272 | tf_op jit(solution)/shard_map/ppermute | solution.py:21
  (186 shorter events, 85.4 us)
Async XLA Ops:
  5.7 32.1 %collective-permute-start.2 = (bf16[160,1152]{1,0:T(8,128)(2,1)}, bf16[160,1152]{1,0:T(8,128)(2,1)S(1)}, u32[]{:S(2)}, u32[]{:S(2)}) collective-permute-start(bf16[160,1152]{1,0:T(8,128)(2,1)} %slice.256.refs_0_), channel_id=1, source_target_pairs={{0,8},{4,12},{8,0},{12,4},{1,9},{5,13},{9,1},{13,5},{2,10},{6,14},... | collective-permute-start | bytes 1105928 | tf_op jit(solution)/shard_map/ppermute | solution.py:64
  12.0 24.4 %collective-permute-start.28 = (bf16[160,768]{1,0:T(8,128)(2,1)S(1)}, bf16[160,768]{1,0:T(8,128)(2,1)}, u32[]{:S(2)}, u32[]{:S(2)}) collective-permute-start(bf16[160,768]{1,0:T(8,128)(2,1)S(1)} %slice.301.refs_0_), channel_id=1, source_target_pairs={{0,8},{4,12},{8,0},{12,4},{1,9},{5,13},{9,1},{13,5},{2,10},{6,14},... | collective-permute-start | bytes 737288 | tf_op jit(solution)/shard_map/ppermute | solution.py:64
  13.4 72.6 %collective-permute-start.12 = (bf16[160,1152]{1,0:T(8,128)(2,1)}, bf16[160,1152]{1,0:T(8,128)(2,1)S(1)}, u32[]{:S(2)}, u32[]{:S(2)}) collective-permute-start(bf16[160,1152]{1,0:T(8,128)(2,1)} %slice.256.refs_0_), channel_id=1, source_target_pairs={{0,4},{4,8},{8,12},{1,5},{5,9},{9,13},{2,6},{6,10},{10,14},{3,7},{... | collective-permute-start | bytes 1105928 | tf_op jit(solution)/shard_map/ppermute | solution.py:64
  16.6 25.0 %collective-permute-start.30 = (bf16[160,768]{1,0:T(8,128)(2,1)S(1)}, bf16[160,768]{1,0:T(8,128)(2,1)S(1)}, u32[]{:S(2)}, u32[]{:S(2)}) collective-permute-start(bf16[160,768]{1,0:T(8,128)(2,1)S(1)} %slice.301.refs_0_), channel_id=1, source_target_pairs={{0,4},{4,8},{8,12},{1,5},{5,9},{9,13},{2,6},{6,10},{10,14},{3,7},{... | collective-permute-start | bytes 737288 | tf_op jit(solution)/shard_map/ppermute | solution.py:64
  19.9 23.1 %collective-permute-start.31 = (bf16[160,768]{1,0:T(8,128)(2,1)S(1)}, bf16[160,768]{1,0:T(8,128)(2,1)S(1)}, u32[]{:S(2)}, u32[]{:S(2)}) collective-permute-start(bf16[160,768]{1,0:T(8,128)(2,1)S(1)} %slice.301.refs_0_), channel_id=1, source_target_pairs={{4,0},{8,4},{12,8},{5,1},{9,5},{13,9},{6,2},{10,6},{14,10},{7,3},{... | collective-permute-start | bytes 737288 | tf_op jit(solution)/shard_map/ppermute | solution.py:64
  36.5 23.0 %collective-permute-start.29 = (bf16[160,768]{1,0:T(8,128)(2,1)}, bf16[160,768]{1,0:T(8,128)(2,1)S(1)}, u32[]{:S(2)}, u32[]{:S(2)}) collective-permute-start(bf16[160,768]{1,0:T(8,128)(2,1)} %collective-permute-done.28), channel_id=1, source_target_pairs={{4,0},{8,12},{5,1},{9,13},{6,2},{10,14},{7,3},{11,15},{20,16},{24,... | collective-permute-start | bytes 737288 | tf_op jit(solution)/shard_map/ppermute | solution.py:65
  38.6 23.9 %collective-permute-start.3 = (bf16[2,4,16,2560]{3,2,1,0:T(8,128)(2,1)S(1)}, bf16[2,4,16,2560]{3,2,1,0:T(8,128)(2,1)S(1)}, u32[]{:S(2)}, u32[]{:S(2)}) collective-permute-start(bf16[2,4,16,2560]{3,2,1,0:T(8,128)(2,1)S(1)} %pad_maximum_fusion.4), channel_id=1, source_target_pairs={{0,4},{4,8},{8,12},{12,0},{1,5},{5,9},{9,13},{13,1},{2,6},{6,10},{... | collective-permute-start | bytes 1966088 | tf_op jit(solution)/shard_map/ppermute | solution.py:21
  41.7 45.6 %collective-permute-start.13 = (bf16[160,1152]{1,0:T(8,128)(2,1)}, bf16[160,1152]{1,0:T(8,128)(2,1)S(1)}, u32[]{:S(2)}, u32[]{:S(2)}) collective-permute-start(bf16[160,1152]{1,0:T(8,128)(2,1)} %slice.256.refs_0_), channel_id=1, source_target_pairs={{4,0},{8,4},{12,8},{5,1},{9,5},{13,9},{6,2},{10,6},{14,10},{7,3},{... | collective-permute-start | bytes 1105928 | tf_op jit(solution)/shard_map/ppermute | solution.py:64
  43.0 42.7 %collective-permute-start.32 = (bf16[160,768]{1,0:T(8,128)(2,1)S(1)}, bf16[160,768]{1,0:T(8,128)(2,1)S(1)}, u32[]{:S(2)}, u32[]{:S(2)}) collective-permute-start(bf16[160,768]{1,0:T(8,128)(2,1)S(1)} %slice.301.refs_0_), channel_id=1, source_target_pairs={{0,16},{16,0},{1,17},{17,1},{2,18},{18,2},{3,19},{19,3},{4,20},{20... | collective-permute-start | bytes 737288 | tf_op jit(solution)/shard_map/ppermute | solution.py:21
  59.5 23.1 %collective-permute-start.21 = (bf16[32,1280]{1,0:T(8,128)(2,1)S(1)}, bf16[32,1280]{1,0:T(8,128)(2,1)S(1)}, u32[]{:S(2)}, u32[]{:S(2)}) collective-permute-start(bf16[32,1280]{1,0:T(8,128)(2,1)S(1)} %pad_maximum_fusion.11), channel_id=1, source_target_pairs={{0,2},{2,0},{1,3},{3,1},{4,6},{6,4},{5,7},{7,5},{8,10},{10,8},{9,1... | collective-permute-start | bytes 245768 | tf_op jit(solution)/shard_map/ppermute | solution.py:21
  85.7 26.9 %collective-permute-start.5 = (bf16[2,16,4,2560]{3,2,1,0:T(4,128)(2,1)}, bf16[2,16,4,2560]{3,2,1,0:T(4,128)(2,1)}, u32[]{:S(2)}, u32[]{:S(2)}) collective-permute-start(bf16[2,16,4,2560]{3,2,1,0:T(4,128)(2,1)} %fusion.26), channel_id=1, source_target_pairs={{0,2},{2,0},{1,3},{3,1},{4,6},{6,4},{5,7},{7,5},{8,10},{10,8},{9,1... | collective-permute-start | bytes 1966088 | tf_op jit(solution)/shard_map/ppermute | solution.py:21
  87.3 31.0 %collective-permute-start.7 = (bf16[16,16,2560]{2,1,0:T(8,128)(2,1)S(1)}, bf16[16,16,2560]{2,1,0:T(8,128)(2,1)}, u32[]{:S(2)}, u32[]{:S(2)}) collective-permute-start(bf16[16,16,2560]{2,1,0:T(8,128)(2,1)S(1)} %bitcast.50), channel_id=1, source_target_pairs={{0,1},{1,0},{2,3},{3,2},{4,5},{5,4},{6,7},{7,6},{8,9},{9,8},{10,11... | collective-permute-start | bytes 3932168 | tf_op jit(solution)/shard_map/ppermute | solution.py:21
  95.8 28.5 %collective-permute-start.8 = (bf16[16,16,2560]{2,1,0:T(8,128)(2,1)S(1)}, bf16[16,16,2560]{2,1,0:T(8,128)(2,1)}, u32[]{:S(2)}, u32[]{:S(2)}) collective-permute-start(bf16[16,16,2560]{2,1,0:T(8,128)(2,1)S(1)} %bitcast.46), channel_id=1, source_target_pairs={{0,1},{1,0},{2,3},{3,2},{4,5},{5,4},{6,7},{7,6},{8,9},{9,8},{10,11... | collective-permute-start | bytes 3932168 | tf_op jit(solution)/shard_map/ppermute | solution.py:21
  101.1 23.6 %collective-permute-start.9 = (bf16[2,4,16,2560]{3,2,1,0:T(8,128)(2,1)S(1)}, bf16[2,4,16,2560]{3,2,1,0:T(8,128)(2,1)}, u32[]{:S(2)}, u32[]{:S(2)}) collective-permute-start(bf16[2,4,16,2560]{3,2,1,0:T(8,128)(2,1)S(1)} %collective-permute-done.3.refs_2_), channel_id=1, source_target_pairs={{0,1},{1,0},{2,3},{3,2},{4,5},{5,4},{6,7},{7,6},{8,9},{9,8},{10,11... | collective-permute-start | bytes 1966088 | tf_op jit(solution)/shard_map/ppermute | solution.py:21
  101.1 24.8 %collective-permute-start.10 = (bf16[2,4,16,2560]{3,2,1,0:T(8,128)(2,1)}, bf16[2,4,16,2560]{3,2,1,0:T(8,128)(2,1)}, u32[]{:S(2)}, u32[]{:S(2)}) collective-permute-start(bf16[2,4,16,2560]{3,2,1,0:T(8,128)(2,1)} %copy-done.8), channel_id=1, source_target_pairs={{0,1},{1,0},{2,3},{3,2},{4,5},{5,4},{6,7},{7,6},{8,9},{9,8},{10,11... | collective-permute-start | bytes 1966088 | tf_op jit(solution)/shard_map/ppermute | solution.py:21
  118.2 58.2 %collective-permute-start.17 = (bf16[480,1152]{1,0:T(8,128)(2,1)}, bf16[480,1152]{1,0:T(8,128)(2,1)}, u32[]{:S(2)}, u32[]{:S(2)}) collective-permute-start(bf16[480,1152]{1,0:T(8,128)(2,1)} %pad_maximum_fusion.refs_1_), channel_id=1, source_target_pairs={{0,2},{2,0},{1,3},{3,1},{4,6},{6,4},{5,7},{7,5},{8,10},{10,8},{9,1... | collective-permute-start | bytes 3317768 | tf_op jit(solution)/shard_map/ppermute | solution.py:21
  124.3 25.3 %collective-permute-start.34 = (bf16[160,768]{1,0:T(8,128)(2,1)S(1)}, bf16[160,768]{1,0:T(8,128)(2,1)S(1)}, u32[]{:S(2)}, u32[]{:S(2)}) collective-permute-start(bf16[160,768]{1,0:T(8,128)(2,1)S(1)} %slice.301.refs_0_), channel_id=1, source_target_pairs={{0,2},{2,0},{1,3},{3,1},{4,6},{6,4},{5,7},{7,5},{8,10},{10,8},{9,1... | collective-permute-start | bytes 737288 | tf_op jit(solution)/shard_map/ppermute | solution.py:21
  124.6 30.3 %collective-permute-start.36 = (bf16[160,768]{1,0:T(8,128)(2,1)}, bf16[160,768]{1,0:T(8,128)(2,1)S(1)}, u32[]{:S(2)}, u32[]{:S(2)}) collective-permute-start(bf16[160,768]{1,0:T(8,128)(2,1)} %copy-done.26), channel_id=1, source_target_pairs={{0,2},{2,0},{1,3},{3,1},{4,6},{6,4},{5,7},{7,5},{8,10},{10,8},{9,1... | collective-permute-start | bytes 737288 | tf_op jit(solution)/shard_map/ppermute | solution.py:21
  125.9 36.9 %collective-permute-start.37 = (bf16[240,768]{1,0:T(8,128)(2,1)S(1)}, bf16[240,768]{1,0:T(8,128)(2,1)S(1)}, u32[]{:S(2)}, u32[]{:S(2)}) collective-permute-start(bf16[240,768]{1,0:T(8,128)(2,1)S(1)} %slice.359), channel_id=1, source_target_pairs={{0,2},{2,0},{1,3},{3,1},{4,6},{6,4},{5,7},{7,5},{8,10},{10,8},{9,1... | collective-permute-start | bytes 1105928 | tf_op jit(solution)/shard_map/ppermute | solution.py:21
  126.1 37.8 %collective-permute-start.38 = (bf16[240,768]{1,0:T(8,128)(2,1)S(1)}, bf16[240,768]{1,0:T(8,128)(2,1)S(1)}, u32[]{:S(2)}, u32[]{:S(2)}) collective-permute-start(bf16[240,768]{1,0:T(8,128)(2,1)S(1)} %slice.360), channel_id=1, source_target_pairs={{0,16},{16,0},{1,17},{17,1},{2,18},{18,2},{3,19},{19,3},{4,20},{20... | collective-permute-start | bytes 1105928 | tf_op jit(solution)/shard_map/ppermute | solution.py:21
  149.6 25.2 %collective-permute-start = (s32[1,1]{1,0:T(1,128)}, s32[1,1]{1,0:T(1,128)}, u32[]{:S(2)}, u32[]{:S(2)}) collective-permute-start(s32[1,1]{1,0:T(1,128)} %param.11), channel_id=1, source_target_pairs={{0,1},{1,0},{2,3},{3,2},{4,5},{5,4},{6,7},{7,6},{8,9},{9,8},{10,11... | collective-permute-start | bytes 20 | tf_op jit(solution)/shard_map/ppermute | solution.py:21
  154.9 20.9 %collective-permute-start.22 = (bf16[64,1280]{1,0:T(8,128)(2,1)S(1)}, bf16[64,1280]{1,0:T(8,128)(2,1)S(1)}, u32[]{:S(2)}, u32[]{:S(2)}) collective-permute-start(bf16[64,1280]{1,0:T(8,128)(2,1)S(1)} %constant_dynamic-update-slice_fusion.refs_0_.refs_4_), channel_id=1, source_target_pairs={{0,4},{4,8},{8,12},{12,0},{1,5},{5,9},{9,13},{13,1},{2,6},{6,10},{... | collective-permute-start | bytes 491528 | tf_op jit(solution)/shard_map/ppermute | solution.py:21
  175.8 36.7 %collective-permute-start.15 = (bf16[480,1152]{1,0:T(8,128)(2,1)}, bf16[480,1152]{1,0:T(8,128)(2,1)S(1)}, u32[]{:S(2)}, u32[]{:S(2)}) collective-permute-start(bf16[480,1152]{1,0:T(8,128)(2,1)} %pad_maximum_fusion.refs_1_), channel_id=1, source_target_pairs={{0,16},{16,0},{1,17},{17,1},{2,18},{18,2},{3,19},{19,3},{4,20},{20... | collective-permute-start | bytes 3317768 | tf_op jit(solution)/shard_map/ppermute | solution.py:21
  176.4 55.0 %collective-permute-start.19 = (bf16[480,1152]{1,0:T(8,128)(2,1)}, bf16[480,1152]{1,0:T(8,128)(2,1)}, u32[]{:S(2)}, u32[]{:S(2)}) collective-permute-start(bf16[480,1152]{1,0:T(8,128)(2,1)} %collective-permute-done.17.refs_5_), channel_id=1, source_target_pairs={{0,16},{16,0},{1,17},{17,1},{2,18},{18,2},{3,19},{19,3},{4,20},{20... | collective-permute-start | bytes 3317768 | tf_op jit(solution)/shard_map/ppermute | solution.py:21
  (49 other events, 764.2 us)
